TPU v7x, 32 devices: a whole 2x2x4 slice. The times are simulated.
32 devices in a mesh: replica: 8 (over z, y), shard: 4 (over x, core).
Axes of the slice: x: 2, y: 2, z: 4, core: 2. Of those that a mesh axis runs over, the one named last changes fastest.
Arguments:
- hidden_in: bfloat16 [4096, 1024], P(('replica', 'shard')), may hold values from -6 to 6
- out_grad: bfloat16 [4096, 1024], P(('replica', 'shard')), may hold values from -6 to 6
- lengths: int32 [32, 4], P(('replica', 'shard')), may hold values from 1 to 64, 128 in all within a row
- norm1_gain: bfloat16 [1024], P('shard'), may hold values from 0.099609375 to 1.8984375
- norm1_bias: bfloat16 [1024], P('shard'), may hold values from -3 to 3
- qkv_weight: bfloat16 [1024, 3072], P('shard'), may hold values from -0.1875 to 0.1875
- query_bias: bfloat16 [1024], P('shard'), may hold values from -3 to 3
- value_bias: bfloat16 [1024], P('shard'), may hold values from -3 to 3
- out_weight: bfloat16 [1024, 1024], P('shard'), may hold values from -0.75 to 0.75
- out_bias: bfloat16 [1024], P('shard'), may hold values from -3 to 3
- norm2_gain: bfloat16 [1024], P('shard'), may hold values from 0.099609375 to 1.8984375
- norm2_bias: bfloat16 [1024], P('shard'), may hold values from -3 to 3
- up_weight: bfloat16 [1024, 4096], P('shard'), may hold values from -0.1875 to 0.1875
- up_bias: bfloat16 [4096], P('shard'), may hold values from -3 to 3
- down_weight: bfloat16 [4096, 1024], P('shard'), may hold values from -0.125 to 0.125
- down_bias: bfloat16 [1024], P('shard'), may hold values from -3 to 3
Outputs:
- hidden_out: bfloat16 [4096, 1024], P(('replica', 'shard'))
- in_grad: bfloat16 [4096, 1024], P(('replica', 'shard'))
- norm1_gain_grad: float32 [1024], P('shard')
- norm1_bias_grad: float32 [1024], P('shard')
- qkv_weight_grad: float32 [1024, 3072], P('shard')
- query_bias_grad: float32 [1024], P('shard')
- value_bias_grad: float32 [1024], P('shard')
- out_weight_grad: float32 [1024, 1024], P('shard')
- out_bias_grad: float32 [1024], P('shard')
- norm2_gain_grad: float32 [1024], P('shard')
- norm2_bias_grad: float32 [1024], P('shard')
- up_weight_grad: float32 [1024, 4096], P('shard')
- up_bias_grad: float32 [4096], P('shard')
- down_weight_grad: float32 [4096, 1024], P('shard')
- down_bias_grad: float32 [1024], P('shard')
Inputs may be any that keep to these rules, and one draw needn't show every extreme that they name: The 4 lengths of each device add up to 128, and the largest of all is 64.
All inputs are finite; a program needn't handle non-finite values.
Results may differ from a plain program's by a relative error of at most 0.018.
Values may be sent and summed in bfloat16 or wider, within the bound.
A program may use at most 192 MiB of HBM per device.

v0:
```python
import functools
import math

import jax
import jax.numpy as jnp
from jax import lax
from jax.experimental import pallas as pl
from jax.experimental.pallas import tpu as pltpu
from jax.sharding import PartitionSpec as P

HEADS = 16
HEAD_DIM = 64


EPSILON = 1e-05
TANH_SCALE = math.sqrt(2.0 / math.pi)
CUBIC = 0.044715


def product(left, right):
    return jnp.dot(left, right, preferred_element_type=jnp.float32)


def left_product(left, right):
    return lax.dot_general(
        left, right, (((0,), (0,)), ((), ())), preferred_element_type=jnp.float32
    )


def right_product(left, right):
    return lax.dot_general(
        left, right, (((1,), (1,)), ((), ())), preferred_element_type=jnp.float32
    )


def column_term(left, right):
    return left_product(left, right)


def gelu_parts(pre_act):
    inner_arg = TANH_SCALE * (pre_act + CUBIC * pre_act * pre_act * pre_act)
    tangent = jnp.tanh(inner_arg)
    gelu_value = 0.5 * pre_act * (1.0 + tangent)
    gelu_slope = 0.5 * (1.0 + tangent) + 0.5 * pre_act * (1.0 - tangent * tangent) * TANH_SCALE * (
        1.0 + 3.0 * CUBIC * pre_act * pre_act
    )
    return (gelu_value, gelu_slope)


def layer_norm(inputs, gain_row, bias_row):
    average = jnp.mean(inputs, axis=-1, keepdims=True)
    centred = inputs - average
    inv_std = lax.rsqrt(jnp.mean(centred * centred, axis=-1, keepdims=True) + EPSILON)
    normed = centred * inv_std
    return (normed * gain_row.astype(jnp.float32) + bias_row.astype(jnp.float32), normed, inv_std)


def norm_back(upstream, normed, inv_std, gain_row):
    scaled = upstream * gain_row.astype(jnp.float32)
    first_term = jnp.mean(scaled, axis=-1, keepdims=True)
    second_term = jnp.mean(scaled * normed, axis=-1, keepdims=True)
    input_grad = inv_std * (scaled - first_term - normed * second_term)
    return (input_grad, jnp.sum(upstream * normed, axis=0), jnp.sum(upstream, axis=0))


def seq_mask(lengths, row_count):
    seq_ends = jnp.cumsum(lengths, axis=-1)
    places = jnp.arange(row_count, dtype=jnp.int32)
    segment = jnp.sum((places[None, :, None] >= seq_ends[:, None, :]).astype(jnp.int32), axis=-1)
    causal = places[None, :] <= places[:, None]
    return (segment[:, :, None] == segment[:, None, :]) & causal[None]


def split_heads(flat_rows, groups):
    return flat_rows.reshape(groups, -1, flat_rows.shape[1] // HEAD_DIM, HEAD_DIM)


def attend_forward(queries, key_rows, values, allowed):
    groups = allowed.shape[0]
    scale_factor = 1.0 / math.sqrt(HEAD_DIM)
    head_q = split_heads(queries, groups)
    head_k = split_heads(key_rows, groups)
    head_v = split_heads(values, groups)
    scores = (
        jnp.einsum("gqhd,gkhd->ghqk", head_q, head_k, preferred_element_type=jnp.float32)
        * scale_factor
    )
    visible = allowed[:, None]
    row_total = jnp.sum(jnp.where(visible, jnp.exp(scores), 0.0), axis=-1, keepdims=True)
    log_total = jnp.log(row_total)
    probs_round = jnp.where(visible, jnp.exp(scores - log_total), 0.0).astype(jnp.bfloat16)
    context = jnp.einsum("ghqk,gkhd->gqhd", probs_round, head_v, preferred_element_type=jnp.float32)
    return (context.reshape(-1, queries.shape[1]).astype(jnp.bfloat16), log_total)


def attend_backward(queries, key_rows, values, allowed, log_total, context_grad):
    groups = allowed.shape[0]
    scale_factor = 1.0 / math.sqrt(HEAD_DIM)
    head_q = split_heads(queries, groups)
    head_k = split_heads(key_rows, groups)
    head_v = split_heads(values, groups)
    head_g = split_heads(context_grad, groups)
    scores = (
        jnp.einsum("gqhd,gkhd->ghqk", head_q, head_k, preferred_element_type=jnp.float32)
        * scale_factor
    )
    visible = allowed[:, None]
    exact_probs = jnp.where(visible, jnp.exp(scores - log_total), 0.0)
    probs_round = exact_probs.astype(jnp.bfloat16)
    prob_grad = jnp.einsum("gqhd,gkhd->ghqk", head_g, head_v, preferred_element_type=jnp.float32)
    value_grad = jnp.einsum(
        "ghqk,gqhd->gkhd", probs_round, head_g, preferred_element_type=jnp.float32
    )
    row_delta = jnp.sum(exact_probs * prob_grad, axis=-1, keepdims=True)
    score_grad = (exact_probs * (prob_grad - row_delta) * scale_factor).astype(jnp.bfloat16)
    query_grad = jnp.einsum(
        "ghqk,gkhd->gqhd", score_grad, head_k, preferred_element_type=jnp.float32
    )
    key_grad = jnp.einsum("ghqk,gqhd->gkhd", score_grad, head_q, preferred_element_type=jnp.float32)
    model_width = queries.shape[1]
    return (
        query_grad.reshape(-1, model_width),
        key_grad.reshape(-1, model_width),
        value_grad.reshape(-1, model_width),
    )


MESH = pl.DeviceIdType.MESH
VMEM_LIMIT = 60 * 1024 * 1024


def push(source, target, send_sem, recv_sem, device):
    return pltpu.make_async_remote_copy(
        src_ref=source,
        dst_ref=target,
        send_sem=send_sem,
        recv_sem=recv_sem,
        device_id=device,
        device_id_type=MESH,
    )


def greet(devices):
    barrier = pltpu.get_barrier_semaphore()
    for device in devices:
        pl.semaphore_signal(barrier, inc=1, device_id=device, device_id_type=MESH)
    pl.semaphore_wait(barrier, len(devices))


def group_peers(replica, me, size):
    return [(replica, lax.rem(me + k, size)) for k in range(1, size)]


class Spread:
    def __init__(self, blocks, replica, me, size, send, recv):
        core = lax.rem(me, 2)
        outer = me // 2
        half = size // 2
        self.partner = (replica, me + 1 - 2 * core)
        self.blocks, self.me, self.send, self.recv = blocks, me, send, recv
        self.size = size
        others = [lax.rem(outer + k, half) for k in range(1, half)]
        self.mates = [2 * j + core for j in others]
        self.far = [2 * j + 1 - core for j in others]
        self.replica = replica
        self.count = half

    def copy(self, k, block, device):
        return push(
            self.blocks.at[block], self.blocks.at[block], self.send.at[k], self.recv.at[block], device
        )

    def start(self):
        for k, mate in enumerate(self.mates):
            self.copy(k, self.me, (self.replica, mate)).start()
        self.copy(self.count, self.me, self.partner).start()

    def forward(self):
        for k, mate in enumerate(self.mates):
            self.copy(k, mate, self.partner).wait_recv()
            self.copy(self.count + 1 + k, mate, self.partner).start()

    def finish(self):
        for block in [self.partner[1]] + self.far:
            self.copy(0, block, self.partner).wait_recv()
        for k in range(len(self.mates)):
            self.copy(k, self.me, self.partner).wait_send()
            self.copy(self.count + 1 + k, self.me, self.partner).wait_send()
        self.copy(self.count, self.me, self.partner).wait_send()


def opening_kernel(size, hid_ref, grad_ref, par_ref, qkv_ref, up_ref,
                   hid_out, grad_out, par_out, qkv_out, up_out,
                   g_send, g_recv, w_send, w_recv, f_send, local_sem):
    replica = lax.axis_index("replica")
    me = lax.axis_index("shard")
    twin = replica + 1 - 2 * lax.rem(replica, 2)
    part = lax.rem(replica, 2)
    core = lax.rem(me, 2)
    outer = me // 2
    half = size // 2
    partner = me + 1 - 2 * core
    greet(group_peers(replica, me, size) + [(twin, me)])
    own = []
    for i, (src, dst) in enumerate(
        ((hid_ref, hid_out), (grad_ref, grad_out), (par_ref, par_out), (qkv_ref, qkv_out), (up_ref, up_out))
    ):
        if i < 3:
            own.append(pltpu.make_async_copy(src.at[0], dst.at[me], local_sem.at[i]))
        else:
            own.append(pltpu.make_async_copy(src.at[me], dst.at[me], local_sem.at[i]))
        own[-1].start()
    spreads = [
        Spread(out, replica, me, size, g_send.at[i], g_recv.at[i])
        for i, out in enumerate((hid_out, grad_out, par_out))
    ]
    own[0].wait()
    own[2].wait()
    spreads[2].start()
    spreads[0].start()
    remote = []
    for k in range(1, half):
        j = lax.rem(outer + k, half)
        remote += [2 * j + core, 2 * j + 1 - core]
    weights = ((qkv_ref, qkv_out), (up_ref, up_out))
    first = []
    for w, (src, dst) in enumerate(weights):
        for t, target in enumerate(remote):
            copy = push(
                src.at[target, part], dst.at[me, part],
                w_send.at[w, t], w_recv.at[w, me, part], (replica, target),
            )
            copy.start()
            first.append(copy)
        for h in range(2):
            copy = push(
                src.at[partner, h], dst.at[me, h],
                w_send.at[w, len(remote) + h], w_recv.at[w, me, h], (replica, partner),
            )
            copy.start()
            first.append(copy)
    own[1].wait()
    spreads[1].start()
    spreads[2].forward()
    spreads[0].forward()
    second = []
    for w, (src, dst) in enumerate(weights):
        for t, source in enumerate(remote):
            arrived = push(
                src.at[source, part], dst.at[source, part],
                w_send.at[w, t], w_recv.at[w, source, part], (replica, source),
            )
            arrived.wait_recv()
            copy = push(
                dst.at[source, part], dst.at[source, part],
                f_send.at[w, t], w_recv.at[w, source, part], (twin, me),
            )
            copy.start()
            second.append(copy)
    spreads[1].forward()
    for w, (src, dst) in enumerate(weights):
        for source in remote:
            push(
                dst.at[source, 1 - part], dst.at[source, 1 - part],
                f_send.at[w, 0], w_recv.at[w, source, 1 - part], (twin, me),
            ).wait_recv()
        for h in range(2):
            push(
                src.at[partner, h], dst.at[partner, h],
                w_send.at[w, 0], w_recv.at[w, partner, h], (replica, partner),
            ).wait_recv()
    for copy in first + second:
        copy.wait_send()
    own[3].wait()
    own[4].wait()
    for spread in spreads:
        spread.finish()


def vmem_specs(count):
    return [pl.BlockSpec(memory_space=pltpu.VMEM)] * count


def opening(size, hidden, upstream, params, qkv_parts, up_parts):
    dma = pltpu.SemaphoreType.DMA
    shape = lambda array: jax.ShapeDtypeStruct((size,) + array.shape[1:], array.dtype)
    arrays = (hidden[None], upstream[None], params[None], qkv_parts, up_parts)
    return pl.pallas_call(
        functools.partial(opening_kernel, size),
        out_shape=tuple(shape(a) for a in arrays),
        in_specs=vmem_specs(5),
        out_specs=tuple(vmem_specs(5)),
        scratch_shapes=[
            dma((3, size)), dma((3, size)), dma((2, size)), dma((2, size, 2)), dma((2, size)), dma((5,)),
        ],
        compiler_params=pltpu.CompilerParams(
            collective_id=0, has_side_effects=True, vmem_limit_bytes=VMEM_LIMIT
        ),
    )(*arrays)


def group_sum_kernel(size, gathers, *refs):
    n = len(gathers)
    half = size // 2
    ins, outs = refs[:n], refs[n : 2 * n]
    scratch = refs[2 * n :]
    replica = lax.axis_index("replica")
    me = lax.axis_index("shard")
    core = lax.rem(me, 2)
    outer = me // 2
    partner = (replica, me + 1 - 2 * core)
    greet(group_peers(replica, me, size))
    order = [lax.rem(outer + k, half) for k in range(1, half)] + [outer]
    work = []
    for i in range(n):
        near, summed, far, p_send, p_recv, x_send, x_recv, g_send, g_recv = scratch[9 * i : 9 * i + 9]
        for k, j in enumerate(order):
            push(
                ins[i].at[2 * j + 1 - core], near.at[j], p_send.at[k], p_recv.at[j], partner
            ).start()
    for i in range(n):
        near, summed, far, p_send, p_recv, x_send, x_recv, g_send, g_recv = scratch[9 * i : 9 * i + 9]
        for k, j in enumerate(order):
            push(ins[i].at[2 * j + 1 - core], near.at[j], p_send.at[k], p_recv.at[j], partner).wait_recv()
            if k < half - 1:
                block = ins[i][2 * j + core].astype(jnp.float32) + near[j].astype(jnp.float32)
                summed[k] = block.astype(jnp.bfloat16)
                push(
                    summed.at[k], far.at[outer], x_send.at[k], x_recv.at[outer], (replica, 2 * j + core)
                ).start()
    spreads = []
    for i in range(n):
        near, summed, far, p_send, p_recv, x_send, x_recv, g_send, g_recv = scratch[9 * i : 9 * i + 9]
        total = ins[i][me].astype(jnp.float32) + near[outer].astype(jnp.float32)
        for k, j in enumerate(order[:-1]):
            push(
                summed.at[k], far.at[j], x_send.at[k], x_recv.at[j], (replica, 2 * j + core)
            ).wait_recv()
            total = total + far[j].astype(jnp.float32)
        if gathers[i]:
            outs[i][me] = total.astype(outs[i].dtype)
            spread = Spread(outs[i], replica, me, size, g_send, g_recv)
            spread.start()
            spreads.append(spread)
        else:
            outs[i][...] = total.astype(outs[i].dtype)
    for spread in spreads:
        spread.forward()
    for spread in spreads:
        spread.finish()
    for i in range(n):
        near, summed, far, p_send, p_recv, x_send, x_recv, g_send, g_recv = scratch[9 * i : 9 * i + 9]
        for k, j in enumerate(order):
            push(ins[i].at[2 * j + 1 - core], near.at[j], p_send.at[k], p_recv.at[j], partner).wait_send()
            if k < half - 1:
                push(
                    summed.at[k], far.at[outer], x_send.at[k], x_recv.at[outer], (replica, 2 * j + core)
                ).wait_send()


def group_sum(size, partials, gathers, collective):
    dma = pltpu.SemaphoreType.DMA
    half = size // 2
    shapes, scratch, blocks = [], [], []
    for partial, gather in zip(partials, gathers):
        block = partial.reshape(size, -1, partial.shape[-1])
        blocks.append(block)
        if gather:
            shapes.append(jax.ShapeDtypeStruct(block.shape, jnp.bfloat16))
        else:
            shapes.append(jax.ShapeDtypeStruct(block.shape[1:], jnp.float32))
        for _ in range(3):
            scratch.append(pltpu.VMEM((half,) + block.shape[1:], jnp.bfloat16))
        scratch += [dma((half,)), dma((half,)), dma((half,)), dma((half,)), dma((size,)), dma((size,))]
    return pl.pallas_call(
        functools.partial(group_sum_kernel, size, gathers),
        out_shape=tuple(shapes),
        in_specs=vmem_specs(len(blocks)),
        out_specs=tuple(vmem_specs(len(blocks))),
        scratch_shapes=scratch,
        compiler_params=pltpu.CompilerParams(
            collective_id=collective, has_side_effects=True, vmem_limit_bytes=VMEM_LIMIT
        ),
    )(*blocks)


KEEP, SWAP, ADD = 0, 1, 2


def closing_kernel(size, ring, modes, *refs):
    n = len(modes)
    ins, outs, lands = refs[:n], refs[n : 2 * n], refs[2 * n : 3 * n]
    swaps = refs[3 * n : 4 * n]
    r_send, r_recv, a_send, a_recv, s_send, s_recv = refs[4 * n :]
    replica = lax.axis_index("replica")
    me = lax.axis_index("shard")
    side = lax.rem(replica, 2)
    depth = replica // 2
    place = (1 - side) * depth + side * (ring - 1 - depth)
    step = 1 - 2 * lax.rem(me, 2)

    def member(position):
        position = lax.rem(position + 2 * ring, ring)
        late = position // (ring // 2)
        return (1 - late) * 2 * position + late * (2 * (ring - 1 - position) + 1)

    after = (member(place + step), me)
    before = (member(place - step), me)
    chunk = lambda hops: lax.rem(place - step * hops + 2 * ring, ring)
    greet(group_peers(replica, me, size) + [after, before])

    def reduce_copy(i, k):
        source = ins[i].at[chunk(1)] if k == 0 else lands[i].at[k - 1]
        return push(source, lands[i].at[k], r_send.at[i, k], r_recv.at[i, k], after)

    for i in range(n):
        reduce_copy(i, 0).start()
    for k in range(ring - 1):
        for i in range(n):
            reduce_copy(i, k).wait_recv()
            mine = ins[i][chunk(k + 2)].astype(jnp.float32)
            total = (mine + lands[i][k].astype(jnp.float32)).astype(lands[i].dtype)
            lands[i][k] = total
            if k < ring - 2:
                reduce_copy(i, k + 1).start()
            elif modes[i] == KEEP:
                outs[i][place] = total

    def swap_copy(i, k, source):
        target = lax.rem(me + k, size)
        return push(
            lands[i].at[ring - 2, target], swaps[i].at[source],
            s_send.at[i, k], s_recv.at[i, source], (replica, target),
        )

    for i in range(n):
        if modes[i] != KEEP:
            for k in range(1, size):
                swap_copy(i, k, me).start()
            swaps[i][me] = lands[i][ring - 2, me]

    def gather_copy(i, k):
        return push(
            outs[i].at[chunk(k)], outs[i].at[chunk(k)], a_send.at[i, k], a_recv.at[i, k], after
        )

    def arrival(i, k):
        return push(
            outs[i].at[chunk(k + 1)], outs[i].at[chunk(k + 1)], a_send.at[i, k], a_recv.at[i, k], after
        )

    order = [i for i in range(n) if modes[i] == KEEP] + [i for i in range(n) if modes[i] != KEEP]
    for i in order:
        if modes[i] != KEEP:
            for k in range(1, size):
                swap_copy(i, size - k, lax.rem(me + k, size)).wait_recv()
            if modes[i] == SWAP:
                outs[i][place] = swaps[i][...]
            else:
                outs[i][place] = jnp.sum(swaps[i][...], axis=0)
        gather_copy(i, 0).start()
    for k in range(ring - 1):
        for i in order:
            arrival(i, k).wait_recv()
            if k < ring - 2:
                gather_copy(i, k + 1).start()
    for i in range(n):
        for k in range(ring - 1):
            reduce_copy(i, k).wait_send()
            gather_copy(i, k).wait_send()
        if modes[i] != KEEP:
            for k in range(1, size):
                swap_copy(i, k, me).wait_send()


def closing(size, ring, arrays, modes):
    dma = pltpu.SemaphoreType.DMA
    n = len(arrays)
    shapes, lands, swaps = [], [], []
    for array, mode in zip(arrays, modes):
        out = array.shape if mode != ADD else array.shape[:1] + array.shape[2:]
        shapes.append(jax.ShapeDtypeStruct(out, array.dtype))
        lands.append(pltpu.VMEM((ring - 1,) + array.shape[1:], array.dtype))
        swaps.append(
            pltpu.VMEM(array.shape[1:] if mode != KEEP else (8, 128), array.dtype)
        )
    return pl.pallas_call(
        functools.partial(closing_kernel, size, ring, modes),
        out_shape=tuple(shapes),
        in_specs=vmem_specs(n),
        out_specs=tuple(vmem_specs(n)),
        scratch_shapes=lands + swaps + [
            dma((n, ring)), dma((n, ring)), dma((n, ring)), dma((n, ring)), dma((n, size)), dma((n, size)),
        ],
        compiler_params=pltpu.CompilerParams(
            collective_id=5, has_side_effects=True, vmem_limit_bytes=VMEM_LIMIT
        ),
    )(*arrays)


def local(
    ring,
    size,
    hidden_in,
    out_grad,
    lengths,
    norm1_gain,
    norm1_bias,
    qkv_weight,
    query_bias,
    value_bias,
    out_weight,
    out_bias,
    norm2_gain,
    norm2_bias,
    up_weight,
    up_bias,
    down_weight,
    down_bias,
):
    me = lax.axis_index("shard")
    rows, width = hidden_in.shape
    band = width // size
    seqs = lengths.shape[1]
    lane_count = max(band, 128)
    wide = lambda vector: jnp.pad(vector, (0, lane_count - vector.shape[0]))
    params = jnp.stack(
        [
            wide(v)
            for v in (
                norm1_gain, norm1_bias, out_bias, norm2_gain, norm2_bias, down_bias,
                lengths[0].astype(jnp.bfloat16), norm1_gain,
            )
        ]
    )
    qkv_parts = qkv_weight.reshape(2, band // 2, 3, size, band).transpose(3, 0, 1, 2, 4)
    qkv_parts = qkv_parts.reshape(size, 2, band // 2, 3 * band)
    ff_band = up_weight.shape[1] // size
    up_parts = up_weight.reshape(2, band // 2, size, ff_band).transpose(2, 0, 1, 3)
    hidden_all, upstream_all, params_all, qkv_all, up_all = opening(
        size, hidden_in, out_grad, params, qkv_parts, up_parts
    )
    hidden_all = hidden_all.reshape(size * rows, width)
    grad_all = upstream_all.reshape(size * rows, width)
    qkv_cols = qkv_all.reshape(width, 3 * band)
    up_cols = up_all.reshape(width, ff_band)
    gain_one, bias_one, outb_full, gain_two, bias_two, downb_full = (
        params_all[:, i, :band].reshape(width) for i in range(6)
    )
    lengths_all = params_all[:, 6, :seqs].astype(jnp.int32)
    mine = lambda array: lax.dynamic_slice_in_dim(array, me * band, band, axis=array.ndim - 1)
    own_rows = lambda array: lax.dynamic_slice_in_dim(array, me * rows, rows, axis=0)

    allowed = seq_mask(lengths_all, rows)
    inputs_wide = hidden_all.astype(jnp.float32)
    first_out, normed_one, inv_one = layer_norm(inputs_wide, gain_one, bias_one)
    first_in = first_out.astype(jnp.bfloat16)
    projected = product(first_in, qkv_cols)
    queries = (projected[:, :band] + query_bias.astype(jnp.float32)).astype(jnp.bfloat16)
    key_rows = projected[:, band : 2 * band].astype(jnp.bfloat16)
    values = (projected[:, 2 * band :] + value_bias.astype(jnp.float32)).astype(jnp.bfloat16)
    context, log_total = attend_forward(queries, key_rows, values, allowed)
    (attended,) = group_sum(
        size, [product(context, out_weight).astype(jnp.bfloat16)], (True,), 1
    )
    residual = (
        inputs_wide
        + attended.reshape(size * rows, width).astype(jnp.float32)
        + outb_full.astype(jnp.float32)
    )
    second_out, normed_two, inv_two = layer_norm(residual, gain_two, bias_two)
    second_in = second_out.astype(jnp.bfloat16)
    pre_act = product(second_in, up_cols) + up_bias.astype(jnp.float32)
    activ_value, gelu_slope = gelu_parts(pre_act)
    activated = activ_value.astype(jnp.bfloat16)
    down_part = product(activated, down_weight).astype(jnp.bfloat16)
    upstream = grad_all.astype(jnp.float32)
    pre_grad = right_product(grad_all, down_weight) * gelu_slope
    pre_round = pre_grad.astype(jnp.bfloat16)
    second_part = right_product(pre_round, up_cols).astype(jnp.bfloat16)
    second_sum, down_sum = group_sum(size, [second_part, down_part], (True, False), 2)
    hidden_out = (own_rows(residual) + down_sum + downb_full.astype(jnp.float32)).astype(
        jnp.bfloat16
    )
    down_grad = column_term(activated, grad_all).astype(jnp.bfloat16)
    up_grad = column_term(second_in, pre_round).astype(jnp.bfloat16)
    second_grad = second_sum.reshape(size * rows, width).astype(jnp.float32)
    norm_two_in, gain2_grad, bias2_grad = norm_back(second_grad, normed_two, inv_two, gain_two)
    resid_grad = upstream + norm_two_in
    resid_round = resid_grad.astype(jnp.bfloat16)
    outw_grad = column_term(context, resid_round).astype(jnp.bfloat16)
    context_grad = right_product(resid_round, out_weight).astype(jnp.bfloat16)
    query_grad, key_grad, value_grad = attend_backward(
        queries, key_rows, values, allowed, log_total, context_grad
    )
    qkv_grad = jnp.concatenate([query_grad, key_grad, value_grad], axis=1).astype(jnp.bfloat16)
    first_part = right_product(qkv_grad, qkv_cols).astype(jnp.bfloat16)
    (first_grad,) = group_sum(size, [first_part], (False,), 3)
    qkvw_grad = column_term(first_in, qkv_grad).astype(jnp.bfloat16)
    norm_one_in, gain1_grad, bias1_grad = norm_back(
        first_grad, own_rows(normed_one), own_rows(inv_one), gain_one
    )
    in_grad = (own_rows(resid_grad) + norm_one_in).astype(jnp.bfloat16)

    owned = jnp.concatenate(
        [
            jnp.sum(query_grad, axis=0),
            jnp.sum(value_grad, axis=0),
            mine(jnp.sum(resid_grad, axis=0)),
            mine(gain2_grad),
            mine(bias2_grad),
            jnp.sum(pre_grad, axis=0),
            mine(jnp.sum(upstream, axis=0)),
        ]
    )
    here = (jnp.arange(size) == me)[:, None]
    small = jnp.concatenate(
        [
            gain1_grad.reshape(size, band),
            bias1_grad.reshape(size, band),
            jnp.where(here, owned[None], 0.0),
        ],
        axis=1,
    )
    count = small.shape[1]
    small = small.reshape(size, ring, 1, count // ring).transpose(1, 0, 2, 3)
    slab = band // ring
    by_owner = lambda array: array.reshape(size, ring, slab, array.shape[1]).transpose(1, 0, 2, 3)
    down_all, outw_all, up_total, qkv_total, small_all = closing(
        size,
        ring,
        [
            down_grad.reshape(ring, -1, width),
            outw_grad.reshape(ring, -1, width),
            by_owner(up_grad),
            by_owner(qkvw_grad),
            small,
        ],
        (KEEP, KEEP, SWAP, SWAP, ADD),
    )
    downw_total = down_all.reshape(down_weight.shape).astype(jnp.float32)
    outw_total = outw_all.reshape(out_weight.shape).astype(jnp.float32)
    upw_total = up_total.transpose(0, 2, 1, 3).reshape(up_weight.shape).astype(jnp.float32)
    qkvw_total = (
        qkv_total.reshape(ring, size, slab, 3, band)
        .transpose(0, 2, 3, 1, 4)
        .reshape(qkv_weight.shape)
        .astype(jnp.float32)
    )
    flat = small_all.reshape(count)
    pieces = []
    offset = 0
    for length in (band, band, band, band, band, band, band, ff_band, band):
        pieces.append(flat[offset : offset + length])
        offset += length
    gain1_t, bias1_t, qbias_t, vbias_t, outb_t, gain2_t, bias2_t, upb_t, downb_t = pieces
    return (
        hidden_out,
        in_grad,
        gain1_t,
        bias1_t,
        qkvw_total,
        qbias_t,
        vbias_t,
        outw_total,
        outb_t,
        gain2_t,
        bias2_t,
        upw_total,
        upb_t,
        downw_total,
        downb_t,
    )


def lanes(start, width):
    return pl.ds(pl.multiple_of(start, 128), width)


def entry_kernel(size, splits, hid_ref, grad_ref, par_ref, qkv_ref, up_ref,
                 hid_out, grad_out, par_out, qkv_out, up_out,
                 g_send, g_recv, w_send, w_recv, f_send, local_sem, own_sem):
    replica = lax.axis_index("replica")
    me = lax.axis_index("shard")
    twin = replica + 1 - 2 * lax.rem(replica, 2)
    part = lax.rem(replica, 2)
    core = lax.rem(me, 2)
    outer = me // 2
    half = size // 2
    partner = me + 1 - 2 * core
    weights = ((qkv_ref, qkv_out), (up_ref, up_out))
    own = []
    for i, (src, dst) in enumerate(((hid_ref, hid_out), (grad_ref, grad_out), (par_ref, par_out))):
        own.append(pltpu.make_async_copy(src.at[0], dst.at[me], local_sem.at[i]))
        own[-1].start()

    def views(w, owner, target, h):
        src, dst = weights[w]
        span = src.shape[2] // splits[w]
        wide = span // size
        for j in range(splits[w]):
            yield (
                j,
                src.at[h, :, lanes(j * span + target * wide, wide)],
                dst.at[owner, h, :, pl.ds(j * wide, wide)],
            )

    for w in range(2):
        for h in range(2):
            for j, source, target in views(w, me, me, h):
                own.append(pltpu.make_async_copy(source, target, own_sem.at[w, h, j]))
                own[-1].start()
    greet(group_peers(replica, me, size) + [(twin, me)])
    spreads = [
        Spread(out, replica, me, size, g_send.at[i], g_recv.at[i])
        for i, out in enumerate((hid_out, grad_out, par_out))
    ]
    own[0].wait()
    own[2].wait()
    spreads[2].start()
    spreads[0].start()
    remote = []
    for k in range(1, half):
        j = lax.rem(outer + k, half)
        remote += [2 * j + core, 2 * j + 1 - core]
    first = []
    for w in range(2):
        for t, target in enumerate(remote):
            for j, source, landing in views(w, me, target, part):
                copy = push(
                    source, landing, w_send.at[w, t, j], w_recv.at[w, me, part, j], (replica, target)
                )
                copy.start()
                first.append(copy)
        for h in range(2):
            for j, source, landing in views(w, me, partner, h):
                copy = push(
                    source, landing, w_send.at[w, len(remote) + h, j], w_recv.at[w, me, h, j],
                    (replica, partner),
                )
                copy.start()
                first.append(copy)
    own[1].wait()
    spreads[1].start()
    spreads[2].forward()
    spreads[0].forward()
    second = []
    for w in range(2):
        dst = weights[w][1]
        for t, source in enumerate(remote):
            for j, view, landing in views(w, source, me, part):
                push(
                    view, landing, w_send.at[w, t, j], w_recv.at[w, source, part, j], (replica, source)
                ).wait_recv()
            copy = push(
                dst.at[source, part], dst.at[source, part],
                f_send.at[w, t], w_recv.at[w, source, part, 0], (twin, me),
            )
            copy.start()
            second.append(copy)
    spreads[1].forward()
    for w in range(2):
        dst = weights[w][1]
        for source in remote:
            push(
                dst.at[source, 1 - part], dst.at[source, 1 - part],
                f_send.at[w, 0], w_recv.at[w, source, 1 - part, 0], (twin, me),
            ).wait_recv()
        for h in range(2):
            for j, view, landing in views(w, partner, me, h):
                push(
                    view, landing, w_send.at[w, 0, j], w_recv.at[w, partner, h, j], (replica, partner)
                ).wait_recv()
    for copy in first + second:
        copy.wait_send()
    for copy in own[3:]:
        copy.wait()
    for spread in spreads:
        spread.finish()


def entry(size, hidden, upstream, params, qkv_weight, up_weight):
    dma = pltpu.SemaphoreType.DMA
    band = qkv_weight.shape[0]
    shape = lambda array: jax.ShapeDtypeStruct((size,) + array.shape[1:], array.dtype)
    gathers = (hidden[None], upstream[None], params[None])
    weights = tuple(w.reshape(2, band // 2, w.shape[1]) for w in (qkv_weight, up_weight))
    outs = tuple(shape(a) for a in gathers) + tuple(
        jax.ShapeDtypeStruct((size, 2, band // 2, w.shape[2] // size), w.dtype) for w in weights
    )
    return pl.pallas_call(
        functools.partial(entry_kernel, size, (3, 1)),
        out_shape=outs,
        in_specs=[pl.BlockSpec(memory_space=pl.ANY)] * 5,
        out_specs=tuple(vmem_specs(5)),
        scratch_shapes=[
            dma((3, size)), dma((3, size)), dma((2, size, 3)), dma((2, size, 2, 3)), dma((2, size)),
            dma((3,)), dma((2, 2, 3)),
        ],
        compiler_params=pltpu.CompilerParams(
            collective_id=0, has_side_effects=True, vmem_limit_bytes=VMEM_LIMIT
        ),
    )(*gathers, *weights)


class Where:
    def __init__(self, size, ring):
        self.size, self.ring = size, ring
        self.replica = lax.axis_index("replica")
        self.me = lax.axis_index("shard")
        self.core = lax.rem(self.me, 2)
        self.outer = self.me // 2
        self.half = size // 2
        self.partner = (self.replica, self.me + 1 - 2 * self.core)
        self.order = [lax.rem(self.outer + k, self.half) for k in range(1, self.half)] + [self.outer]
        side = lax.rem(self.replica, 2)
        depth = self.replica // 2
        self.place = (1 - side) * depth + side * (ring - 1 - depth)
        self.step = 1 - 2 * self.core
        self.after = (self.member(self.place + self.step), self.me)
        self.before = (self.member(self.place - self.step), self.me)

    def member(self, position):
        ring = self.ring
        position = lax.rem(position + 2 * ring, ring)
        late = position // (ring // 2)
        return (1 - late) * 2 * position + late * (2 * (ring - 1 - position) + 1)

    def chunk(self, hops):
        return lax.rem(self.place - self.step * hops + 2 * self.ring, self.ring)


class Ring:
    def __init__(self, where, i, source, land, out, swap, sems, mode, pieces=1):
        self.where, self.source, self.land, self.out, self.swap = where, source, land, out, swap
        self.r_send, self.r_recv, self.a_send, self.a_recv, self.s_send, self.s_recv = (
            sem.at[i] for sem in sems
        )
        self.mode, self.pieces = mode, pieces
        self.last = where.ring - 2

    def block(self, position):
        return self.source.at[:, position] if self.mode == SWAP else self.source.at[position]

    def reduce_copy(self, k):
        source = self.block(self.where.chunk(1)) if k == 0 else self.land.at[k - 1]
        return push(source, self.land.at[k], self.r_send.at[k], self.r_recv.at[k], self.where.after)

    def swap_copy(self, k, source):
        where = self.where
        target = lax.rem(where.me + k, where.size)
        return push(
            self.land.at[self.last, target], self.swap.at[source],
            self.s_send.at[k], self.s_recv.at[source], (where.replica, target),
        )

    def gather_copy(self, k, hops):
        part = self.out.at[self.where.chunk(hops)]
        return push(part, part, self.a_send.at[k], self.a_recv.at[k], self.where.after)

    def start(self):
        self.reduce_copy(0).start()

    def reduce_step(self, k):
        where, land = self.where, self.land
        self.reduce_copy(k).wait_recv()
        position = where.chunk(k + 2)
        mine = self.source[:, position] if self.mode == SWAP else self.source[position]
        total = (mine.astype(jnp.float32) + land[k].astype(jnp.float32)).astype(land.dtype)
        land[k] = total
        if k < self.last:
            self.reduce_copy(k + 1).start()
        elif self.mode == KEEP:
            self.out[where.place] = total
            self.gather_copy(0, 0).start()
        else:
            for step in range(1, where.size):
                self.swap_copy(step, where.me).start()
            self.swap[where.me] = land[k, where.me]

    def turn(self):
        where = self.where
        if self.mode == KEEP:
            return
        for k in range(1, where.size):
            self.swap_copy(where.size - k, lax.rem(where.me + k, where.size)).wait_recv()
        if self.mode == ADD:
            self.out[where.place] = jnp.sum(self.swap[...], axis=0)
        else:
            wide = self.land.shape[-1] // self.pieces
            for s in range(where.size):
                for j in range(self.pieces):
                    start = (j * where.size + s) * wide
                    self.out[where.place, :, start : start + wide] = self.swap[
                        s, :, j * wide : (j + 1) * wide
                    ]
        self.gather_copy(0, 0).start()

    def gather_step(self, k):
        self.gather_copy(k, k + 1).wait_recv()
        if k < self.last:
            self.gather_copy(k + 1, k + 1).start()

    def stages(self):
        steps = [functools.partial(self.reduce_step, k) for k in range(self.last + 1)]
        if self.mode != KEEP:
            steps.append(self.turn)
        return steps + [functools.partial(self.gather_step, k) for k in range(self.last + 1)]

    def drain(self):
        for k in range(self.last + 1):
            self.reduce_copy(k).wait_send()
            self.gather_copy(k, k).wait_send()
        if self.mode != KEEP:
            for k in range(1, self.where.size):
                self.swap_copy(k, self.where.me).wait_send()


class GroupSum:
    def __init__(self, where, source, near, summed, far, sems):
        self.where, self.source, self.near, self.summed, self.far = where, source, near, summed, far
        self.p_send, self.p_recv, self.x_send, self.x_recv = sems

    def near_copy(self, k):
        j = self.where.order[k]
        return push(
            self.source.at[2 * j + 1 - self.where.core], self.near.at[j],
            self.p_send.at[k], self.p_recv.at[j], self.where.partner,
        )

    def far_copy(self, k, landing):
        where = self.where
        return push(
            self.summed.at[k], self.far.at[landing], self.x_send.at[k], self.x_recv.at[landing],
            (where.replica, 2 * where.order[k] + where.core),
        )

    def send(self, k):
        self.near_copy(k).start()

    def reduce(self, k):
        where = self.where
        j = where.order[k]
        self.near_copy(k).wait_recv()
        block = self.source[2 * j + where.core].astype(jnp.float32) + self.near[j].astype(jnp.float32)
        self.summed[k] = block.astype(jnp.bfloat16)
        self.far_copy(k, where.outer).start()

    def arrive(self):
        self.near_copy(self.where.half - 1).wait_recv()
        for k in range(self.where.half - 1):
            self.far_copy(k, self.where.order[k]).wait_recv()

    def tile(self, rows):
        where = self.where
        total = self.source[where.me, rows].astype(jnp.float32) + self.near[
            where.outer, rows
        ].astype(jnp.float32)
        for j in where.order[:-1]:
            total = total + self.far[j, rows].astype(jnp.float32)
        return total

    def drain(self):
        for k in range(self.where.half):
            self.near_copy(k).wait_send()
            if k < self.where.half - 1:
                self.far_copy(k, self.where.outer).wait_send()


TILE = 16


def tiles(count, body):
    @pl.loop(0, count // TILE)
    def _(t):
        body(pl.ds(pl.multiple_of(t * TILE, TILE), TILE))


def fold(value):
    return jnp.sum(value.reshape(TILE // 8, 8, value.shape[-1]), axis=0)


def row_stats(inputs):
    average = jnp.mean(inputs, axis=-1, keepdims=True)
    centred = inputs - average
    inv_std = lax.rsqrt(jnp.mean(centred * centred, axis=-1, keepdims=True) + EPSILON)
    return (centred * inv_std, inv_std)


def row_back(upstream, normed, inv_std, gain_row):
    scaled = upstream * gain_row
    first_term = jnp.mean(scaled, axis=-1, keepdims=True)
    second_term = jnp.mean(scaled * normed, axis=-1, keepdims=True)
    return inv_std * (scaled - first_term - normed * second_term)


def back_kernel(size, ring,
                second_ref, down_ref, dgrad_ref, ugrad_ref, resid_ref, grad_ref, hid_ref,
                q_ref, k_ref, v_ref, allow_ref, ctx_ref, outw_ref, first_ref, qkvw_ref,
                vec_ref, upb_ref,
                hidden_out, in_out, down_out, outw_out, up_out, qkv_out, small_out,
                near_a, summed_a, far_a, near_b, summed_b, far_b, near_c, summed_c, far_c,
                ssum, fpart, rgrad, rround, qkvg, outg, qkvwg, small, acc, bias,
                land_d, land_o, land_u, land_q, land_s, swap_u, swap_q, swap_s,
                p_send, p_recv, x_send, x_recv, g_send, g_recv,
                r_send, r_recv, a_send, a_recv, s_send, s_recv):
    where = Where(size, ring)
    me, replica = where.me, where.replica
    rows, width = hid_ref.shape
    band = q_ref.shape[2]
    slab = band // ring
    scale_factor = 1.0 / math.sqrt(HEAD_DIM)
    greet(group_peers(replica, me, size) + [where.after, where.before])
    sems = (r_send, r_recv, a_send, a_recv, s_send, s_recv)
    down_ring = Ring(where, 0, dgrad_ref, land_d, down_out, None, sems, KEEP)
    up_ring = Ring(where, 1, ugrad_ref, land_u, up_out, swap_u, sems, SWAP)
    outw_ring = Ring(where, 2, outg, land_o, outw_out, None, sems, KEEP)
    qkv_ring = Ring(where, 3, qkvwg, land_q, qkv_out, swap_q, sems, SWAP, 3)
    small_ring = Ring(where, 4, small, land_s, small_out, swap_s, sems, ADD)
    sums = []
    for i, buffers in enumerate(
        (
            (second_ref, near_a, summed_a, far_a),
            (down_ref, near_b, summed_b, far_b),
            (fpart, near_c, summed_c, far_c),
        )
    ):
        sums.append(
            GroupSum(where, *buffers, (p_send.at[i], p_recv.at[i], x_send.at[i], x_recv.at[i]))
        )
    second_sum, down_sum, first_sum = sums
    half = where.half

    for k in range(half):
        second_sum.send(k)
    up_ring.start()
    down_ring.start()
    early = []
    late_up, late_down = up_ring.stages(), down_ring.stages()
    while late_up or late_down:
        if late_up:
            early.append(late_up.pop(0))
        if late_down:
            early.append(late_down.pop(0))

    def serve(count):
        for _ in range(count):
            if early:
                early.pop(0)()

    for k in range(half - 1):
        second_sum.reduce(k)
    for k in range(half):
        down_sum.send(k)
    acc[...] = jnp.zeros_like(acc)
    bias[...] = jnp.zeros_like(bias)
    small[...] = jnp.zeros_like(small)
    second_sum.arrive()

    def second_total(part):
        ssum[me, part] = second_sum.tile(part).astype(jnp.bfloat16)

    tiles(rows, second_total)
    spread = Spread(ssum, replica, me, size, g_send, g_recv)
    spread.start()
    for k in range(half - 1):
        down_sum.reduce(k)
    serve(2)

    def norm_two(block):
        def body(part):
            normed, inv_std = row_stats(resid_ref[block, part])
            upper = ssum[block, part].astype(jnp.float32)
            total = grad_ref[block, part].astype(jnp.float32) + row_back(
                upper, normed, inv_std, vec_ref[1:2]
            )
            rgrad[block, part] = total
            rround[block, part] = total.astype(jnp.bfloat16)
            acc[0] += fold(upper * normed)
            acc[1] += fold(upper)
            acc[2] += fold(total)

        tiles(rows, body)

    norm_two(me)
    spread.forward()
    spread.finish()
    for k in range(1, size):
        norm_two(lax.rem(me + k, size))
    serve(2)

    lane = lax.broadcasted_iota(jnp.int32, (rows, 128), 1)
    sides = [(lane < HEAD_DIM), (lane >= HEAD_DIM)]
    masks = [side.astype(jnp.float32).astype(jnp.bfloat16) for side in sides]

    def block_back(block):
        context_grad = right_product(rround[block], outw_ref[...]).astype(jnp.bfloat16)
        visible = allow_ref[block] > 0.5
        for pair in range(band // 128):
            cut = slice(pair * 128, (pair + 1) * 128)
            query, key, value = q_ref[block, :, cut], k_ref[block, :, cut], v_ref[block, :, cut]
            upper = context_grad[:, cut]
            parts = []
            for mask in masks:
                scores = right_product(query * mask, key) * scale_factor
                total = jnp.sum(jnp.where(visible, jnp.exp(scores), 0.0), axis=-1, keepdims=True)
                probs = jnp.where(visible, jnp.exp(scores - jnp.log(total)), 0.0)
                prob_grad = right_product(upper * mask, value)
                delta = jnp.sum(probs * prob_grad, axis=-1, keepdims=True)
                score_grad = (probs * (prob_grad - delta) * scale_factor).astype(jnp.bfloat16)
                parts.append(
                    (
                        product(score_grad, key),
                        left_product(score_grad, query),
                        left_product(probs.astype(jnp.bfloat16), upper),
                    )
                )
            for j in range(3):
                grad = jnp.where(sides[0], parts[0][j], parts[1][j])
                start = j * band + pair * 128
                qkvg[block, :, start : start + 128] = grad.astype(jnp.bfloat16)
                if j != 1:
                    bias[:, start : start + 128] += jnp.sum(
                        grad.reshape(rows // 8, 8, 128), axis=0
                    )
        fpart[block] = right_product(qkvg[block], qkvw_ref[...]).astype(jnp.bfloat16)

    for k in range(half):
        block_back(2 * where.order[k] + 1 - where.core)
        first_sum.send(k)
        if k % 2 == 0:
            serve(1)
    for k in range(half):
        block_back(2 * where.order[k] + where.core)
        if k < half - 1:
            first_sum.reduce(k)
    serve(2)

    flat = lambda value: value.reshape(size * rows, value.shape[-1])

    @pl.loop(0, width // 256)
    def _(t):
        cut = lanes(t * 256, 256)
        grad = left_product(flat(ctx_ref[...]), flat(rround[:, :, cut]))
        outg[:, :, cut] = grad.astype(jnp.bfloat16).reshape(ring, slab, 256)

    outw_ring.start()

    @pl.loop(0, size)
    def _(t):
        grad = left_product(flat(first_ref[:, :, lanes(t * band, band)]), flat(qkvg[...]))
        qkvwg[t] = grad.astype(jnp.bfloat16).reshape(ring, slab, 3 * band)

    qkv_ring.start()
    serve(2)
    first_sum.arrive()

    def norm_one(part):
        normed, inv_std = row_stats(hid_ref[part].astype(jnp.float32))
        upper = first_sum.tile(part)
        total = rgrad[me, part] + row_back(upper, normed, inv_std, vec_ref[0:1])
        in_out[part] = total.astype(jnp.bfloat16)
        acc[3] += fold(upper * normed)
        acc[4] += fold(upper)

    tiles(rows, norm_one)
    down_sum.arrive()

    def finish_hidden(part):
        total = resid_ref[me, part] + down_sum.tile(part) + vec_ref[2:3]
        hidden_out[part] = total.astype(jnp.bfloat16)

    tiles(rows, finish_hidden)

    span = small.shape[3]

    def put(owner, start, row):
        for t in range(row.shape[1] // 128):
            position = start + t * 128
            small[position // span, owner, :, position % span : position % span + 128] = row[
                :, t * 128 : (t + 1) * 128
            ]

    for i in range(2):
        line = jnp.sum(acc[3 + i], axis=0, keepdims=True)
        for s in range(size):
            put(s, i * band, line[:, s * band : (s + 1) * band])
    start = 2 * band
    line = jnp.sum(bias[...], axis=0, keepdims=True)
    put(me, start, line[:, :band])
    put(me, start + band, line[:, 2 * band :])
    start += 2 * band
    for i in (2, 0, 1):
        put(me, start, jnp.sum(acc[i, :, lanes(me * band, band)], axis=0, keepdims=True))
        start += band
    put(me, start, upb_ref[...])
    start += upb_ref.shape[1]
    put(me, start, vec_ref[3:4, lanes(me * band, band)])
    small_ring.start()

    rest = [ring_.stages() for ring_ in (outw_ring, qkv_ring, small_ring)]
    while early or any(rest):
        serve(2)
        for stages in rest:
            if stages:
                stages.pop(0)()
    spread_free = (second_sum, down_sum, first_sum, down_ring, up_ring, outw_ring, qkv_ring, small_ring)
    for part in spread_free:
        part.drain()


def back(size, ring, arrays, small_count):
    dma = pltpu.SemaphoreType.DMA
    (second, down, dgrad, ugrad, resid, grads, hidden, q, k, v, allow, ctx, outw, first, qkvw, vec,
     upb) = arrays
    rows, width = hidden.shape
    band = q.shape[2]
    slab = band // ring
    half = size // 2
    ff_band = ugrad.shape[3]
    b16, f32 = jnp.bfloat16, jnp.float32
    vm = pltpu.VMEM
    scratch = [vm((half, rows, width), b16)] * 9
    scratch += [
        vm((size, rows, width), b16),
        vm((size, rows, width), b16),
        vm((size, rows, width), f32),
        vm((size, rows, width), b16),
        vm((size, rows, 3 * band), b16),
        vm((ring, slab, width), b16),
        vm((size, ring, slab, 3 * band), b16),
        vm((ring, size, 1, small_count // ring), f32),
        vm((5, 8, width), f32),
        vm((8, 3 * band), f32),
        vm((ring - 1,) + dgrad.shape[1:], b16),
        vm((ring - 1, slab, width), b16),
        vm((ring - 1, size, slab, ff_band), b16),
        vm((ring - 1, size, slab, 3 * band), b16),
        vm((ring - 1, size, 1, small_count // ring), f32),
        vm((size, slab, ff_band), b16),
        vm((size, slab, 3 * band), b16),
        vm((size, 1, small_count // ring), f32),
    ]
    scratch += [dma((3, half))] * 4 + [dma((size,))] * 2 + [dma((5, ring))] * 4 + [dma((5, size))] * 2
    shape = jax.ShapeDtypeStruct
    outs = (
        shape((rows, width), b16),
        shape((rows, width), b16),
        shape(dgrad.shape, b16),
        shape((ring, slab, width), b16),
        shape((ring, slab, size * ff_band), b16),
        shape((ring, slab, 3 * width), b16),
        shape((ring, 1, small_count // ring), f32),
    )
    return pl.pallas_call(
        functools.partial(back_kernel, size, ring),
        out_shape=outs,
        in_specs=vmem_specs(len(arrays)),
        out_specs=tuple(vmem_specs(len(outs))),
        scratch_shapes=scratch,
        compiler_params=pltpu.CompilerParams(
            collective_id=2, has_side_effects=True, vmem_limit_bytes=VMEM_LIMIT
        ),
    )(*arrays)


def fused(
    ring,
    size,
    hidden_in,
    out_grad,
    lengths,
    norm1_gain,
    norm1_bias,
    qkv_weight,
    query_bias,
    value_bias,
    out_weight,
    out_bias,
    norm2_gain,
    norm2_bias,
    up_weight,
    up_bias,
    down_weight,
    down_bias,
):
    rows, width = hidden_in.shape
    band = width // size
    seqs = lengths.shape[1]
    ff_band = up_weight.shape[1] // size
    params = jnp.concatenate(
        [
            norm1_gain, norm1_bias, out_bias, norm2_gain, norm2_bias, down_bias,
            jnp.pad(lengths[0].astype(jnp.bfloat16), (0, band - seqs)), norm1_gain,
        ]
    ).reshape(8, band)
    hidden_all, upstream_all, params_all, qkv_all, up_all = entry(
        size, hidden_in, out_grad, params, qkv_weight, up_weight
    )
    hidden_all = hidden_all.reshape(size * rows, width)
    grad_all = upstream_all.reshape(size * rows, width)
    qkv_cols = qkv_all.reshape(width, 3 * band)
    up_cols = up_all.reshape(width, ff_band)
    gain_one, bias_one, outb_full, gain_two, bias_two, downb_full = (
        params_all[:, i, :band].reshape(width) for i in range(6)
    )
    lengths_all = params_all[:, 6, :seqs].astype(jnp.int32)

    allowed = seq_mask(lengths_all, rows)
    inputs_wide = hidden_all.astype(jnp.float32)
    first_out, _, _ = layer_norm(inputs_wide, gain_one, bias_one)
    first_in = first_out.astype(jnp.bfloat16)
    projected = product(first_in, qkv_cols)
    queries = (projected[:, :band] + query_bias.astype(jnp.float32)).astype(jnp.bfloat16)
    key_rows = projected[:, band : 2 * band].astype(jnp.bfloat16)
    values = (projected[:, 2 * band :] + value_bias.astype(jnp.float32)).astype(jnp.bfloat16)
    by_block = lambda array: array.reshape(size, rows, array.shape[-1])
    allow = allowed.astype(jnp.float32)
    context = attend(by_block(queries), by_block(key_rows), by_block(values), allow)
    (attended,) = group_sum(
        size,
        [product(context.reshape(size * rows, band), out_weight).astype(jnp.bfloat16)],
        (True,),
        1,
    )
    residual = (
        inputs_wide
        + attended.reshape(size * rows, width).astype(jnp.float32)
        + outb_full.astype(jnp.float32)
    )
    second_out, _, _ = layer_norm(residual, gain_two, bias_two)
    second_in = second_out.astype(jnp.bfloat16)
    pre_act = product(second_in, up_cols) + up_bias.astype(jnp.float32)
    activ_value, gelu_slope = gelu_parts(pre_act)
    activated = activ_value.astype(jnp.bfloat16)
    down_part = product(activated, down_weight).astype(jnp.bfloat16)
    upstream = grad_all.astype(jnp.float32)
    pre_grad = right_product(grad_all, down_weight) * gelu_slope
    pre_round = pre_grad.astype(jnp.bfloat16)
    second_part = right_product(pre_round, up_cols).astype(jnp.bfloat16)
    down_grad = column_term(activated, grad_all).astype(jnp.bfloat16)
    up_grad = column_term(second_in, pre_round).astype(jnp.bfloat16)
    vectors = jnp.stack(
        [
            gain_one.astype(jnp.float32),
            gain_two.astype(jnp.float32),
            downb_full.astype(jnp.float32),
            jnp.sum(upstream, axis=0),
        ]
    )
    slab = band // ring
    lengths_out = (band, band, band, band, band, band, band, ff_band, band)
    hidden_out, in_grad, down_all, outw_all, up_total, qkv_total, small_all = back(
        size,
        ring,
        (
            by_block(second_part),
            by_block(down_part),
            down_grad.reshape(ring, -1, width),
            up_grad.reshape(size, ring, slab, ff_band),
            by_block(residual),
            by_block(grad_all),
            hidden_in,
            by_block(queries),
            by_block(key_rows),
            by_block(values),
            allow,
            context,
            out_weight,
            by_block(first_in),
            qkv_cols,
            vectors,
            jnp.sum(pre_grad, axis=0)[None],
        ),
        sum(lengths_out),
    )
    final = lambda array, like: array.reshape(like.shape).astype(jnp.float32)
    flat = small_all.reshape(-1)
    pieces = []
    offset = 0
    for length in lengths_out:
        pieces.append(flat[offset : offset + length])
        offset += length
    gain1_t, bias1_t, qbias_t, vbias_t, outb_t, gain2_t, bias2_t, upb_t, downb_t = pieces
    return (
        hidden_out,
        in_grad,
        gain1_t,
        bias1_t,
        final(qkv_total, qkv_weight),
        qbias_t,
        vbias_t,
        final(outw_all, out_weight),
        outb_t,
        gain2_t,
        bias2_t,
        final(up_total, up_weight),
        upb_t,
        final(down_all, down_weight),
        downb_t,
    )


def attend_kernel(q_ref, k_ref, v_ref, allow_ref, ctx_ref):
    rows, band = q_ref.shape[1:]
    lane = lax.broadcasted_iota(jnp.int32, (rows, 128), 1)
    sides = [(lane < HEAD_DIM), (lane >= HEAD_DIM)]
    masks = [side.astype(jnp.float32).astype(jnp.bfloat16) for side in sides]

    @pl.loop(0, q_ref.shape[0])
    def _(block):
        visible = allow_ref[block] > 0.5
        for pair in range(band // 128):
            cut = slice(pair * 128, (pair + 1) * 128)
            query, key, value = q_ref[block, :, cut], k_ref[block, :, cut], v_ref[block, :, cut]
            parts = []
            for mask in masks:
                scores = right_product(query * mask, key) * (1.0 / math.sqrt(HEAD_DIM))
                total = jnp.sum(jnp.where(visible, jnp.exp(scores), 0.0), axis=-1, keepdims=True)
                probs = jnp.where(visible, jnp.exp(scores - jnp.log(total)), 0.0)
                parts.append(product(probs.astype(jnp.bfloat16), value))
            ctx_ref[block, :, cut] = jnp.where(sides[0], parts[0], parts[1]).astype(jnp.bfloat16)


def attend(queries, key_rows, values, allow):
    return pl.pallas_call(
        attend_kernel,
        out_shape=jax.ShapeDtypeStruct(queries.shape, queries.dtype),
        in_specs=vmem_specs(4),
        out_specs=vmem_specs(1)[0],
    )(queries, key_rows, values, allow)


def choose(ring, size, hidden_in, *rest):
    rows, width = hidden_in.shape
    band = width // size
    aligned = width % size == 0 and band % 256 == 0 and band % (16 * ring) == 0
    body = fused if aligned and rows % 128 == 0 and size % 2 == 0 and ring % 2 == 0 else local
    return body(ring, size, hidden_in, *rest)


def solution(mesh):
    in_specs = (
        P(("replica", "shard"), None),
        P(("replica", "shard"), None),
        P(("replica", "shard"), None),
        P("shard"),
        P("shard"),
        P("shard", None),
        P("shard"),
        P("shard"),
        P("shard", None),
        P("shard"),
        P("shard"),
        P("shard"),
        P("shard", None),
        P("shard"),
        P("shard", None),
        P("shard"),
    )
    out_specs = (
        P(("replica", "shard"), None),
        P(("replica", "shard"), None),
        P("shard"),
        P("shard"),
        P("shard", None),
        P("shard"),
        P("shard"),
        P("shard", None),
        P("shard"),
        P("shard"),
        P("shard"),
        P("shard", None),
        P("shard"),
        P("shard", None),
        P("shard"),
    )
    body = functools.partial(choose, mesh.shape["replica"], mesh.shape["shard"])
    return jax.shard_map(body, mesh=mesh, in_specs=in_specs, out_specs=out_specs, check_vma=False)
```

profile of v0, /device:TPU:0, one launch (start us, length us, event | category | flops | bytes accessed | tf_op | source)
XLA Modules:
  0.0 285.1 jit_solution(12790257028274505147)
XLA Ops:
  0.7 0.8 convert_bitcast_fusion
  1.5 0.7 convert_element_type.208
  2.1 0.7 convert_element_type.210
  2.8 0.7 convert_element_type.224
  3.5 0.8 dynamic-update-slice
  4.3 0.8 dynamic-update-slice.1
  5.1 0.8 dynamic-update-slice.2
  6.0 0.8 dynamic-update-slice.3
  6.8 0.8 dynamic-update-slice.4
  7.6 0.8 dynamic-update-slice.5
  8.5 0.2 dynamic-update-slice.6
  8.7 0.8 dynamic-update-slice.7
  9.5 0.6 broadcast_in_dim_reshape.3.par_ref
  10.1 40.8 %shard_map.271 = (bf16[4,128,1024]{2,1,0:T(8,128)(2,1)}, bf16[4,128,1024]{2,1,0:T(8,128)(2,1)}, bf16[4,8,256]{2,1,0:T(8,128)(2,1)}, bf16[4,2,128,768]{3,2,1,0:T(8,128)(2,1)}, bf16[4,2,128,1024]{3,2,1,0:T(8,128)(2,1)}) custom-call(bf16[1,128,1024]{2,1,0:T(8,128)(2,1)} %bitcast.94, bf16[1,128,1024]{2,1,0:T(8,128)(2,1)} %bitcast.96, ...), custom_call_target="tpu_custom_call" | custom-call | tf_op jit(solution)/shard_map/pallas_call | solution.py:791
  50.9 0.8 slice_convert_fusion.6
  51.7 0.2 reduce_window_sum.17
  52.0 1.9 convert_reduce_fusion
  53.8 0.4 fusion.2
  54.3 0.6 pad_maximum_fusion.vec_ref
  54.9 0.8 and_convert_fusion.allow_ref
  55.8 0.4 fusion.5.first_ref
  56.2 1.0 fusion.27
  57.3 0.7 slice.102
  58.0 0.9 fusion.17
  58.9 6.6 %shard_map.272.ctx_ref = bf16[4,128,256]{2,1,0:T(8,128)(2,1)} custom-call(bf16[4,128,256]{2,1,0:T(8,128)(2,1)} %bitcast.84, bf16[4,128,256]{2,1,0:T(8,128)(2,1)} %bitcast.80, bf16[4,128,256]{2,1,0:T(8,128)(2,1)} %bitcast.82, f32[4,128,128]{2,1,0:T(8,128)} %and_convert_fusion.allow_ref), custom_call_target="tpu_custom_call" | custom-call | tf_op jit(solution)/shard_map/pallas_call | solution.py:1426
  65.5 2.5 convolution_convert_fusion.4
  68.0 21.7 %shard_map.273 = bf16[4,128,1024]{2,1,0:T(8,128)(2,1)} custom-call(bf16[4,128,1024]{2,1,0:T(8,128)(2,1)} %bitcast.78), custom_call_target="tpu_custom_call" | custom-call | tf_op jit(solution)/shard_map/pallas_call | solution.py:375
  89.8 1.6 fusion.23
  91.4 0.3 multiply_reduce_fusion
  91.8 0.5 fusion.16
  92.2 0.5 copy-done.1
  92.7 0.4 add_convert_fusion
  93.1 1.2 copy-done.12
  94.3 1.3 fusion.28
  95.6 2.5 convolution_convert_fusion.2
  98.1 3.0 %fusion.26 = (f32[1024]{0:T(1024)}, bf16[512,1024]{1,0:T(8,128)(2,1)S(1)}) fusion(f32[512,1024]{1,0:T(8,128)S(1)} %fusion.28, f32[1024]{0:T(1024)S(1)} %convert_element_type.224, bf16[512,1024]{1,0:T(8,128)(2,1)S(1)} %bitcast.75, bf16[1024,1024]{1,0:T(8,128)(2,1)S(1)} %copy-done), kind=kOutput, calls=%fused_computation.65 | convolution fusion | flops 1084750848 | bytes 6299648 | tf_op jit(solution)/shard_map/dot_general | solution.py:31
  101.1 3.0 %convolution_convert_fusion.1 = bf16[1024,1024]{1,0:T(8,128)(2,1)} fusion(bf16[512,1024]{1,0:T(8,128)(2,1)S(1)} %bitcast.76, f32[512,1024]{1,0:T(8,128)S(1)} %fusion.28, f32[1024]{0:T(1024)S(1)} %convert_element_type.224), kind=kOutput, calls=%fused_computation.30 | convolution fusion | flops 1080033280 | bytes 5246976 | tf_op jit(solution)/shard_map/dot_general | solution.py:25
  104.1 2.3 convolution_convert_fusion.3
  106.3 2.6 convolution_convert_fusion
  109.0 162.3 %shard_map.274 = (bf16[128,1024]{1,0:T(8,128)(2,1)}, bf16[128,1024]{1,0:T(8,128)(2,1)}, bf16[8,128,1024]{2,1,0:T(8,128)(2,1)}, bf16[8,32,1024]{2,1,0:T(8,128)(2,...) custom-call(bf16[4,128,1024]{2,1,0:T(8,128)(2,1)} %bitcast.93, ...), custom_call_target="tpu_custom_call" | custom-call | tf_op jit(solution)/shard_map/pallas_call | solution.py:1255
  271.3 1.4 slice.87
  272.7 1.4 fusion.25
  274.1 2.1 bitcast_convert_fusion.3
  276.3 2.1 bitcast_convert_fusion.2
  278.4 2.6 bitcast_convert_fusion.1
  281.1 2.6 bitcast_convert_fusion
  283.7 0.7 copy.41
  284.4 0.7 copy.42
  (34 shorter events, 0.3 us)
Async XLA Ops:
  0.6 94.9 %copy-start = (bf16[1024,1024]{1,0:T(8,128)(2,1)S(1)}, bf16[1024,1024]{1,0:T(8,128)(2,1)}, u32[]{:S(2)}) copy-start(bf16[1024,1024]{1,0:T(8,128)(2,1)} %param.30) | copy-start | bytes 6291460
  50.9 3.0 %copy-start.2 = (bf16[4,128,1024]{2,1,0:T(8,128)(2,1)S(1)}, bf16[4,128,1024]{2,1,0:T(8,128)(2,1)}, u32[]{:S(2)}) copy-start(bf16[4,128,1024]{2,1,0:T(8,128)(2,1)} %get-tuple-element.28) | copy-start | bytes 3145732
  50.9 3.4 %copy-start.11 = (bf16[4,8,256]{2,1,0:T(8,128)(2,1)S(1)}, bf16[4,8,256]{2,1,0:T(8,128)(2,1)}, u32[]{:S(2)}) copy-start(bf16[4,8,256]{2,1,0:T(8,128)(2,1)} %get-tuple-element.29) | copy-start | bytes 49156
  53.8 2.4 copy-start.7
  56.2 1.1 copy-start.4
  91.4 1.3 copy-start.1
  92.7 1.6 copy-start.12
  95.6 2.5 copy-start.3
  271.3 5.0 %copy-start.8 = (bf16[8,32,3072]{2,1,0:T(8,128)(2,1)S(1)}, bf16[8,32,3072]{2,1,0:T(8,128)(2,1)}, u32[]{:S(2)}) copy-start(bf16[8,32,3072]{2,1,0:T(8,128)(2,1)} %get-tuple-element.35) | copy-start | bytes 4718596
  276.3 2.1 copy-start.6
  278.4 2.6 copy-start.5
  281.0 2.6 copy-start.10
  281.1 3.3 %copy-start.9 = (bf16[128,1024]{1,0:T(8,128)(2,1)S(1)}, bf16[128,1024]{1,0:T(8,128)(2,1)}, u32[]{:S(2)}) copy-start(bf16[128,1024]{1,0:T(8,128)(2,1)} %get-tuple-element.84) | copy-start | bytes 786436
where the time goes:
time: 286 us; the launch traced here: 285 us
  Pallas kernels  231 us (81%)
  other arithmetic  21.3 us (7%)
  matrix products  18.1 us (6%)
  local copies, waits for them, and re-layouts  13.4 us (5%)
    pallas_call x1, Pallas kernels, back(): pl.pallas_call(functools.partial(back_kernel, size, ring), out_shape=outs...  162 us
    pallas_call x1, Pallas kernels, entry(): pl.pallas_call(functools.partial(entry_kernel, size, (3, 1)), out_shape=o...  40.8 us
    pallas_call x1, Pallas kernels, group_sum(): pl.pallas_call(functools.partial(group_sum_kernel, size, gathers), out_sh...  21.7 us
    convert_element_type x4, other arithmetic, fused(): final = lambda array, like: array.reshape(like.shape).astype(jnp.float32)  9.51 us
    unnamed x35, local copies, waits for them, and re-layouts  8.36 us
    dot_general x4, matrix products, product(): return jnp.dot(left, right, preferred_element_type=jnp.float32)  7.28 us
    pallas_call x1, Pallas kernels, attend(): pl.pallas_call(attend_kernel, out_shape=jax.ShapeDtypeStruct(queries.shap...  6.61 us

commit v1 on v0

--- a/solution.py
+++ b/solution.py
@@ -682,35 +682,41 @@
                  g_send, g_recv, w_send, w_recv, f_send, local_sem, own_sem):
     replica = lax.axis_index("replica")
     me = lax.axis_index("shard")
-    twin = replica + 1 - 2 * lax.rem(replica, 2)
-    part = lax.rem(replica, 2)
+    low = lax.rem(replica, 2)
+    high = lax.rem(replica // 2, 2)
+    part = low + 2 * high
     core = lax.rem(me, 2)
     outer = me // 2
     half = size // 2
     partner = me + 1 - 2 * core
+    flips = ((1, 0), (0, 1), (1, 1))
+    twins = [replica + a * (1 - 2 * low) + 2 * b * (1 - 2 * high) for a, b in flips]
+    theirs = [
+        (low + a * (1 - 2 * low)) + 2 * (high + b * (1 - 2 * high)) for a, b in flips
+    ]
     weights = ((qkv_ref, qkv_out), (up_ref, up_out))
     own = []
     for i, (src, dst) in enumerate(((hid_ref, hid_out), (grad_ref, grad_out), (par_ref, par_out))):
         own.append(pltpu.make_async_copy(src.at[0], dst.at[me], local_sem.at[i]))
         own[-1].start()
 
-    def views(w, owner, target, h):
+    def views(w, owner, target, which):
         src, dst = weights[w]
         span = src.shape[2] // splits[w]
         wide = span // size
         for j in range(splits[w]):
             yield (
                 j,
-                src.at[h, :, lanes(j * span + target * wide, wide)],
-                dst.at[owner, h, :, pl.ds(j * wide, wide)],
+                src.at[which, :, lanes(j * span + target * wide, wide)],
+                dst.at[owner, which, :, pl.ds(j * wide, wide)],
             )
 
+    full = slice(None)
     for w in range(2):
-        for h in range(2):
-            for j, source, target in views(w, me, me, h):
-                own.append(pltpu.make_async_copy(source, target, own_sem.at[w, h, j]))
-                own[-1].start()
-    greet(group_peers(replica, me, size) + [(twin, me)])
+        for j, source, target in views(w, me, me, full):
+            own.append(pltpu.make_async_copy(source, target, own_sem.at[w, j]))
+            own[-1].start()
+    greet(group_peers(replica, me, size) + [(twin, me) for twin in twins])
     spreads = [
         Spread(out, replica, me, size, g_send.at[i], g_recv.at[i])
         for i, out in enumerate((hid_out, grad_out, par_out))
@@ -732,14 +738,13 @@
                 )
                 copy.start()
                 first.append(copy)
-        for h in range(2):
-            for j, source, landing in views(w, me, partner, h):
-                copy = push(
-                    source, landing, w_send.at[w, len(remote) + h, j], w_recv.at[w, me, h, j],
-                    (replica, partner),
-                )
-                copy.start()
-                first.append(copy)
+        for j, source, landing in views(w, me, partner, full):
+            copy = push(
+                source, landing, w_send.at[w, len(remote), j], w_recv.at[w, me, 0, j],
+                (replica, partner),
+            )
+            copy.start()
+            first.append(copy)
     own[1].wait()
     spreads[1].start()
     spreads[2].forward()
@@ -752,25 +757,26 @@
                 push(
                     view, landing, w_send.at[w, t, j], w_recv.at[w, source, part, j], (replica, source)
                 ).wait_recv()
-            copy = push(
-                dst.at[source, part], dst.at[source, part],
-                f_send.at[w, t], w_recv.at[w, source, part, 0], (twin, me),
-            )
-            copy.start()
-            second.append(copy)
+            for m, twin in enumerate(twins):
+                copy = push(
+                    dst.at[source, part], dst.at[source, part],
+                    f_send.at[w, t, m], w_recv.at[w, source, part, 0], (twin, me),
+                )
+                copy.start()
+                second.append(copy)
     spreads[1].forward()
     for w in range(2):
         dst = weights[w][1]
         for source in remote:
+            for m, twin in enumerate(twins):
+                push(
+                    dst.at[source, theirs[m]], dst.at[source, theirs[m]],
+                    f_send.at[w, 0, m], w_recv.at[w, source, theirs[m], 0], (twin, me),
+                ).wait_recv()
+        for j, view, landing in views(w, partner, me, full):
             push(
-                dst.at[source, 1 - part], dst.at[source, 1 - part],
-                f_send.at[w, 0], w_recv.at[w, source, 1 - part, 0], (twin, me),
+                view, landing, w_send.at[w, 0, j], w_recv.at[w, partner, 0, j], (replica, partner)
             ).wait_recv()
-        for h in range(2):
-            for j, view, landing in views(w, partner, me, h):
-                push(
-                    view, landing, w_send.at[w, 0, j], w_recv.at[w, partner, h, j], (replica, partner)
-                ).wait_recv()
     for copy in first + second:
         copy.wait_send()
     for copy in own[3:]:
@@ -784,9 +790,9 @@
     band = qkv_weight.shape[0]
     shape = lambda array: jax.ShapeDtypeStruct((size,) + array.shape[1:], array.dtype)
     gathers = (hidden[None], upstream[None], params[None])
-    weights = tuple(w.reshape(2, band // 2, w.shape[1]) for w in (qkv_weight, up_weight))
+    weights = tuple(w.reshape(4, band // 4, w.shape[1]) for w in (qkv_weight, up_weight))
     outs = tuple(shape(a) for a in gathers) + tuple(
-        jax.ShapeDtypeStruct((size, 2, band // 2, w.shape[2] // size), w.dtype) for w in weights
+        jax.ShapeDtypeStruct((size, 4, band // 4, w.shape[2] // size), w.dtype) for w in weights
     )
     return pl.pallas_call(
         functools.partial(entry_kernel, size, (3, 1)),
@@ -794,8 +800,8 @@
         in_specs=[pl.BlockSpec(memory_space=pl.ANY)] * 5,
         out_specs=tuple(vmem_specs(5)),
         scratch_shapes=[
-            dma((3, size)), dma((3, size)), dma((2, size, 3)), dma((2, size, 2, 3)), dma((2, size)),
-            dma((3,)), dma((2, 2, 3)),
+            dma((3, size)), dma((3, size)), dma((2, size, 3)), dma((2, size, 4, 3)),
+            dma((2, size, 3)), dma((3,)), dma((2, 3)),
         ],
         compiler_params=pltpu.CompilerParams(
             collective_id=0, has_side_effects=True, vmem_limit_bytes=VMEM_LIMIT
@@ -855,8 +861,14 @@
         )
 
     def gather_copy(self, k, hops):
-        part = self.out.at[self.where.chunk(hops)]
+        part = self.spot(self.where.chunk(hops))
         return push(part, part, self.a_send.at[k], self.a_recv.at[k], self.where.after)
+
+    def spot(self, position):
+        if self.mode != ADD:
+            return self.out.at[position]
+        wide = self.land.shape[-1]
+        return self.out.at[:, lanes(position * wide, wide)]
 
     def start(self):
         self.reduce_copy(0).start()
@@ -866,7 +878,7 @@
         self.reduce_copy(k).wait_recv()
         position = where.chunk(k + 2)
         mine = self.source[:, position] if self.mode == SWAP else self.source[position]
-        total = (mine.astype(jnp.float32) + land[k].astype(jnp.float32)).astype(land.dtype)
+        total = (mine.astype(ADDS) + land[k].astype(ADDS)).astype(land.dtype)
         land[k] = total
         if k < self.last:
             self.reduce_copy(k + 1).start()
@@ -885,7 +897,7 @@
         for k in range(1, where.size):
             self.swap_copy(where.size - k, lax.rem(where.me + k, where.size)).wait_recv()
         if self.mode == ADD:
-            self.out[where.place] = jnp.sum(self.swap[...], axis=0)
+            self.spot(where.place)[...] = jnp.sum(self.swap[...], axis=0)
         else:
             wide = self.land.shape[-1] // self.pieces
             for s in range(where.size):
@@ -968,6 +980,10 @@
 
 
 TILE = 16
+PAIR_SERVE = 0
+SPLIT = 2
+ADDS = jnp.float32
+LATE_RATE = 1
 
 
 def tiles(count, body):
@@ -995,10 +1011,13 @@
 
 
 def back_kernel(size, ring,
-                second_ref, down_ref, dgrad_ref, ugrad_ref, resid_ref, grad_ref, hid_ref,
+                act_ref, pre_ref, grad_ref, vec_ref, upb_ref,
+                sec_hbm, upw_hbm, dnw_hbm, resid_hbm, hid_hbm,
+                q_hbm, k_hbm, v_hbm, allow_hbm, ctx_hbm, outw_hbm, first_hbm, qkvw_hbm,
+                hidden_out, in_out, down_out, outw_out, up_out, qkv_out, small_out,
+                sec_ref, upw_ref, dnw_ref, resid_ref, hid_ref,
                 q_ref, k_ref, v_ref, allow_ref, ctx_ref, outw_ref, first_ref, qkvw_ref,
-                vec_ref, upb_ref,
-                hidden_out, in_out, down_out, outw_out, up_out, qkv_out, small_out,
+                second_ref, down_ref, dgrad_ref, ugrad_ref, load_sem,
                 near_a, summed_a, far_a, near_b, summed_b, far_b, near_c, summed_c, far_c,
                 ssum, fpart, rgrad, rround, qkvg, outg, qkvwg, small, acc, bias,
                 land_d, land_o, land_u, land_q, land_s, swap_u, swap_q, swap_s,
@@ -1010,13 +1029,58 @@
     band = q_ref.shape[2]
     slab = band // ring
     scale_factor = 1.0 / math.sqrt(HEAD_DIM)
+    loads = [
+        pltpu.make_async_copy(source, target, load_sem.at[i])
+        for i, (source, target) in enumerate(
+            (
+                (sec_hbm, sec_ref), (upw_hbm, upw_ref), (resid_hbm, resid_ref), (dnw_hbm, dnw_ref),
+                (ctx_hbm, ctx_ref), (outw_hbm, outw_ref), (q_hbm, q_ref), (k_hbm, k_ref),
+                (v_hbm, v_ref), (allow_hbm, allow_ref), (qkvw_hbm, qkvw_ref), (first_hbm, first_ref),
+                (hid_hbm, hid_ref),
+            )
+        )
+    ]
+    for load in loads:
+        load.start()
     greet(group_peers(replica, me, size) + [where.after, where.before])
+    flat = lambda value: value.reshape(size * rows, value.shape[-1])
     sems = (r_send, r_recv, a_send, a_recv, s_send, s_recv)
-    down_ring = Ring(where, 0, dgrad_ref, land_d, down_out, None, sems, KEEP)
-    up_ring = Ring(where, 1, ugrad_ref, land_u, up_out, swap_u, sems, SWAP)
-    outw_ring = Ring(where, 2, outg, land_o, outw_out, None, sems, KEEP)
-    qkv_ring = Ring(where, 3, qkvwg, land_q, qkv_out, swap_q, sems, SWAP, 3)
-    small_ring = Ring(where, 4, small, land_s, small_out, swap_s, sems, ADD)
+    index = iter(range(r_send.shape[0]))
+
+    def rings(source, land, out, swap, mode, count, pieces=1):
+        made = []
+        deep = out.shape[1] // count
+        for n in range(count):
+            part = pl.ds(n * deep, deep)
+            views = (
+                (source.at[:, part], land.at[:, part], out.at[:, part], None)
+                if mode == KEEP
+                else (source.at[:, :, part], land.at[:, :, part], out.at[:, part], swap.at[:, part])
+            )
+            made.append(Ring(where, next(index), *views, sems, mode, pieces))
+        return made
+
+    down_rings = rings(dgrad_ref, land_d, down_out, None, KEEP, SPLIT)
+    up_rings = rings(ugrad_ref, land_u, up_out, swap_u, SWAP, SPLIT)
+    outw_rings = rings(outg, land_o, outw_out, None, KEEP, 1)
+    qkv_rings = rings(qkvwg, land_q, qkv_out, swap_q, SWAP, SPLIT, 3)
+    small_ring = Ring(where, next(index), small, land_s, small_out, swap_s, sems, ADD)
+    all_rings = down_rings + up_rings + outw_rings + qkv_rings + [small_ring]
+
+    def launch(made):
+        for ring_ in made:
+            ring_.start()
+
+    def woven(queues):
+        queues = [list(queue) for queue in queues]
+        order = []
+        while any(queues):
+            for queue in queues:
+                if queue:
+                    order.append(queue.pop(0))
+        return order
+
+    stages_of = lambda made: [ring_.stages() for ring_ in made]
     sums = []
     for i, buffers in enumerate(
         (
@@ -1031,30 +1095,59 @@
     second_sum, down_sum, first_sum = sums
     half = where.half
 
+    deep = dgrad_ref.shape[1]
+
+    def down_chunk(hops):
+        position = where.chunk(hops)
+        grad = left_product(act_ref[:, lanes(position * deep, deep)], flat(grad_ref[...]))
+        dgrad_ref[position] = grad.astype(jnp.bfloat16)
+
+    def own_rows(block):
+        return pl.ds(pl.multiple_of(block * rows, rows), rows)
+
+    def second_block(block):
+        grad = right_product(pre_ref[own_rows(block)], upw_ref[...])
+        second_ref[block] = grad.astype(jnp.bfloat16)
+
+    def down_block(block):
+        part = product(act_ref[own_rows(block)], dnw_ref[...])
+        down_ref[block] = part.astype(jnp.bfloat16)
+
+    down_chunk(1)
+    launch(down_rings)
+    loads[0].wait()
+
+    @pl.loop(0, size)
+    def _(t):
+        grad = left_product(sec_ref[:, lanes(t * band, band)], pre_ref[...])
+        ugrad_ref[t] = grad.astype(jnp.bfloat16).reshape(ugrad_ref.shape[1:])
+
+    launch(up_rings)
+    loads[1].wait()
     for k in range(half):
+        second_block(2 * where.order[k] + 1 - where.core)
         second_sum.send(k)
-    up_ring.start()
-    down_ring.start()
-    early = []
-    late_up, late_down = up_ring.stages(), down_ring.stages()
-    while late_up or late_down:
-        if late_up:
-            early.append(late_up.pop(0))
-        if late_down:
-            early.append(late_down.pop(0))
+
+    @pl.loop(2, ring + 1)
+    def _(hops):
+        down_chunk(hops)
+
+    for k in range(half):
+        second_block(2 * where.order[k] + where.core)
+    ffn_rings = [ring_ for pair in zip(down_rings, up_rings) for ring_ in pair]
+    early = woven(stages_of(ffn_rings))
 
     def serve(count):
-        for _ in range(count):
+        for _ in range(count * SPLIT):
             if early:
                 early.pop(0)()
 
     for k in range(half - 1):
         second_sum.reduce(k)
-    for k in range(half):
-        down_sum.send(k)
     acc[...] = jnp.zeros_like(acc)
     bias[...] = jnp.zeros_like(bias)
     small[...] = jnp.zeros_like(small)
+    serve(2)
     second_sum.arrive()
 
     def second_total(part):
@@ -1063,9 +1156,8 @@
     tiles(rows, second_total)
     spread = Spread(ssum, replica, me, size, g_send, g_recv)
     spread.start()
-    for k in range(half - 1):
-        down_sum.reduce(k)
-    serve(2)
+    loads[2].wait()
+    serve(1)
 
     def norm_two(block):
         def body(part):
@@ -1083,11 +1175,40 @@
         tiles(rows, body)
 
     norm_two(me)
+    serve(1)
     spread.forward()
+    serve(1)
     spread.finish()
     for k in range(1, size):
         norm_two(lax.rem(me + k, size))
-    serve(2)
+        serve(1)
+
+    loads[4].wait()
+
+    @pl.loop(0, width // 256)
+    def _(t):
+        cut = lanes(t * 256, 256)
+        grad = left_product(flat(ctx_ref[...]), flat(rround[:, :, cut]))
+        outg[:, :, cut] = grad.astype(jnp.bfloat16).reshape(ring, slab, 256)
+
+    launch(outw_rings)
+    loads[3].wait()
+    for k in range(half):
+        down_block(2 * where.order[k] + 1 - where.core)
+        down_sum.send(k)
+    for k in range(half):
+        down_block(2 * where.order[k] + where.core)
+    for k in range(half - 1):
+        down_sum.reduce(k)
+    outw_stages = woven(stages_of(outw_rings))
+    merged = []
+    for i, stage in enumerate(early):
+        merged.append(stage)
+        if i % (2 * SPLIT) == 2 * SPLIT - 1 and outw_stages:
+            merged.append(outw_stages.pop(0))
+    early[:] = merged + outw_stages
+    serve(1)
+
 
     lane = lax.broadcasted_iota(jnp.int32, (rows, 128), 1)
     sides = [(lane < HEAD_DIM), (lane >= HEAD_DIM)]
@@ -1096,62 +1217,66 @@
     def block_back(block):
         context_grad = right_product(rround[block], outw_ref[...]).astype(jnp.bfloat16)
         visible = allow_ref[block] > 0.5
-        for pair in range(band // 128):
-            cut = slice(pair * 128, (pair + 1) * 128)
-            query, key, value = q_ref[block, :, cut], k_ref[block, :, cut], v_ref[block, :, cut]
-            upper = context_grad[:, cut]
-            parts = []
-            for mask in masks:
-                scores = right_product(query * mask, key) * scale_factor
-                total = jnp.sum(jnp.where(visible, jnp.exp(scores), 0.0), axis=-1, keepdims=True)
-                probs = jnp.where(visible, jnp.exp(scores - jnp.log(total)), 0.0)
-                prob_grad = right_product(upper * mask, value)
-                delta = jnp.sum(probs * prob_grad, axis=-1, keepdims=True)
-                score_grad = (probs * (prob_grad - delta) * scale_factor).astype(jnp.bfloat16)
-                parts.append(
-                    (
-                        product(score_grad, key),
-                        left_product(score_grad, query),
-                        left_product(probs.astype(jnp.bfloat16), upper),
-                    )
-                )
-            for j in range(3):
-                grad = jnp.where(sides[0], parts[0][j], parts[1][j])
+        cuts = [slice(pair * 128, (pair + 1) * 128) for pair in range(band // 128)]
+        heads = [(cut, mask) for cut in cuts for mask in masks]
+        keys = {cut.start: k_ref[block, :, cut] for cut in cuts}
+        scores = [
+            right_product(q_ref[block, :, cut] * mask, keys[cut.start]) * scale_factor
+            for cut, mask in heads
+        ]
+        prob_grads = [
+            right_product(context_grad[:, cut] * mask, v_ref[block, :, cut]) for cut, mask in heads
+        ]
+        totals = [
+            jnp.sum(jnp.where(visible, jnp.exp(score), 0.0), axis=-1, keepdims=True) for score in scores
+        ]
+        probs = [
+            jnp.where(visible, jnp.exp(score - jnp.log(total)), 0.0)
+            for score, total in zip(scores, totals)
+        ]
+        rounded = [prob.astype(jnp.bfloat16) for prob in probs]
+        deltas = [
+            jnp.sum(prob * grad, axis=-1, keepdims=True) for prob, grad in zip(probs, prob_grads)
+        ]
+        score_grads = [
+            (prob * (grad - delta) * scale_factor).astype(jnp.bfloat16)
+            for prob, grad, delta in zip(probs, prob_grads, deltas)
+        ]
+        groups = [
+            [product(sg, keys[cut.start]) for sg, (cut, _) in zip(score_grads, heads)],
+            [left_product(sg, q_ref[block, :, cut]) for sg, (cut, _) in zip(score_grads, heads)],
+            [left_product(pr, context_grad[:, cut]) for pr, (cut, _) in zip(rounded, heads)],
+        ]
+        for j, group in enumerate(groups):
+            for pair in range(band // 128):
+                grad = jnp.where(sides[0], group[2 * pair], group[2 * pair + 1])
                 start = j * band + pair * 128
                 qkvg[block, :, start : start + 128] = grad.astype(jnp.bfloat16)
                 if j != 1:
                     bias[:, start : start + 128] += jnp.sum(
                         grad.reshape(rows // 8, 8, 128), axis=0
                     )
+        serve(PAIR_SERVE)
         fpart[block] = right_product(qkvg[block], qkvw_ref[...]).astype(jnp.bfloat16)
 
+    for load in loads[5:]:
+        load.wait()
     for k in range(half):
         block_back(2 * where.order[k] + 1 - where.core)
         first_sum.send(k)
-        if k % 2 == 0:
-            serve(1)
+        serve(1)
     for k in range(half):
         block_back(2 * where.order[k] + where.core)
         if k < half - 1:
             first_sum.reduce(k)
-    serve(2)
-
-    flat = lambda value: value.reshape(size * rows, value.shape[-1])
-
-    @pl.loop(0, width // 256)
-    def _(t):
-        cut = lanes(t * 256, 256)
-        grad = left_product(flat(ctx_ref[...]), flat(rround[:, :, cut]))
-        outg[:, :, cut] = grad.astype(jnp.bfloat16).reshape(ring, slab, 256)
-
-    outw_ring.start()
+        serve(1)
 
     @pl.loop(0, size)
     def _(t):
         grad = left_product(flat(first_ref[:, :, lanes(t * band, band)]), flat(qkvg[...]))
         qkvwg[t] = grad.astype(jnp.bfloat16).reshape(ring, slab, 3 * band)
 
-    qkv_ring.start()
+    launch(qkv_rings)
     serve(2)
     first_sum.arrive()
 
@@ -1164,6 +1289,7 @@
         acc[4] += fold(upper)
 
     tiles(rows, norm_one)
+    serve(1)
     down_sum.arrive()
 
     def finish_hidden(part):
@@ -1171,6 +1297,7 @@
         hidden_out[part] = total.astype(jnp.bfloat16)
 
     tiles(rows, finish_hidden)
+    serve(1)
 
     span = small.shape[3]
 
@@ -1198,29 +1325,39 @@
     put(me, start, vec_ref[3:4, lanes(me * band, band)])
     small_ring.start()
 
-    rest = [ring_.stages() for ring_ in (outw_ring, qkv_ring, small_ring)]
-    while early or any(rest):
-        serve(2)
-        for stages in rest:
-            if stages:
-                stages.pop(0)()
-    spread_free = (second_sum, down_sum, first_sum, down_ring, up_ring, outw_ring, qkv_ring, small_ring)
-    for part in spread_free:
+    late = woven(stages_of(qkv_rings + [small_ring]))
+    share = max(1, round(len(early) / max(1, len(late)) * LATE_RATE))
+    while early or late:
+        for _ in range(share):
+            if early:
+                early.pop(0)()
+        for _ in range(LATE_RATE):
+            if late:
+                late.pop(0)()
+    for part in sums + all_rings:
         part.drain()
 
 
 def back(size, ring, arrays, small_count):
     dma = pltpu.SemaphoreType.DMA
-    (second, down, dgrad, ugrad, resid, grads, hidden, q, k, v, allow, ctx, outw, first, qkvw, vec,
-     upb) = arrays
-    rows, width = hidden.shape
-    band = q.shape[2]
+    (act, pre, grads, vec, upb) = arrays[:5]
+    moved = arrays[5:]
+    rows, width = moved[4].shape
+    band = moved[5].shape[2]
     slab = band // ring
     half = size // 2
-    ff_band = ugrad.shape[3]
+    ff_band = act.shape[1]
     b16, f32 = jnp.bfloat16, jnp.float32
     vm = pltpu.VMEM
-    scratch = [vm((half, rows, width), b16)] * 9
+    scratch = [vm(array.shape, array.dtype) for array in moved]
+    scratch += [
+        vm((size, rows, width), b16),
+        vm((size, rows, width), b16),
+        vm((ring, ff_band // ring, width), b16),
+        vm((size, ring, slab, ff_band), b16),
+        dma((len(moved),)),
+    ]
+    scratch += [vm((half, rows, width), b16)] * 9
     scratch += [
         vm((size, rows, width), b16),
         vm((size, rows, width), b16),
@@ -1232,7 +1369,7 @@
         vm((ring, size, 1, small_count // ring), f32),
         vm((5, 8, width), f32),
         vm((8, 3 * band), f32),
-        vm((ring - 1,) + dgrad.shape[1:], b16),
+        vm((ring - 1, ff_band // ring, width), b16),
         vm((ring - 1, slab, width), b16),
         vm((ring - 1, size, slab, ff_band), b16),
         vm((ring - 1, size, slab, 3 * band), b16),
@@ -1241,21 +1378,21 @@
         vm((size, slab, 3 * band), b16),
         vm((size, 1, small_count // ring), f32),
     ]
-    scratch += [dma((3, half))] * 4 + [dma((size,))] * 2 + [dma((5, ring))] * 4 + [dma((5, size))] * 2
+    scratch += [dma((3, half))] * 4 + [dma((size,))] * 2 + [dma((8, ring))] * 4 + [dma((8, size))] * 2
     shape = jax.ShapeDtypeStruct
     outs = (
         shape((rows, width), b16),
         shape((rows, width), b16),
-        shape(dgrad.shape, b16),
+        shape((ring, ff_band // ring, width), b16),
         shape((ring, slab, width), b16),
         shape((ring, slab, size * ff_band), b16),
         shape((ring, slab, 3 * width), b16),
-        shape((ring, 1, small_count // ring), f32),
+        shape((1, small_count), f32),
     )
     return pl.pallas_call(
         functools.partial(back_kernel, size, ring),
         out_shape=outs,
-        in_specs=vmem_specs(len(arrays)),
+        in_specs=vmem_specs(5) + [pl.BlockSpec(memory_space=pl.ANY)] * len(moved),
         out_specs=tuple(vmem_specs(len(outs))),
         scratch_shapes=scratch,
         compiler_params=pltpu.CompilerParams(
@@ -1288,12 +1425,13 @@
     band = width // size
     seqs = lengths.shape[1]
     ff_band = up_weight.shape[1] // size
-    params = jnp.concatenate(
-        [
+    params = layer_rows(
+        (
             norm1_gain, norm1_bias, out_bias, norm2_gain, norm2_bias, down_bias,
-            jnp.pad(lengths[0].astype(jnp.bfloat16), (0, band - seqs)), norm1_gain,
-        ]
-    ).reshape(8, band)
+            jnp.pad(lengths[0].astype(jnp.bfloat16), (0, band - seqs)),
+        ),
+        8,
+    )
     hidden_all, upstream_all, params_all, qkv_all, up_all = entry(
         size, hidden_in, out_grad, params, qkv_weight, up_weight
     )
@@ -1333,20 +1471,17 @@
     pre_act = product(second_in, up_cols) + up_bias.astype(jnp.float32)
     activ_value, gelu_slope = gelu_parts(pre_act)
     activated = activ_value.astype(jnp.bfloat16)
-    down_part = product(activated, down_weight).astype(jnp.bfloat16)
     upstream = grad_all.astype(jnp.float32)
     pre_grad = right_product(grad_all, down_weight) * gelu_slope
     pre_round = pre_grad.astype(jnp.bfloat16)
-    second_part = right_product(pre_round, up_cols).astype(jnp.bfloat16)
-    down_grad = column_term(activated, grad_all).astype(jnp.bfloat16)
-    up_grad = column_term(second_in, pre_round).astype(jnp.bfloat16)
-    vectors = jnp.stack(
-        [
+    vectors = layer_rows(
+        (
             gain_one.astype(jnp.float32),
             gain_two.astype(jnp.float32),
             downb_full.astype(jnp.float32),
             jnp.sum(upstream, axis=0),
-        ]
+        ),
+        8,
     )
     slab = band // ring
     lengths_out = (band, band, band, band, band, band, band, ff_band, band)
@@ -1354,12 +1489,15 @@
         size,
         ring,
         (
-            by_block(second_part),
-            by_block(down_part),
-            down_grad.reshape(ring, -1, width),
-            up_grad.reshape(size, ring, slab, ff_band),
+            activated,
+            pre_round,
+            by_block(grad_all),
+            vectors,
+            jnp.sum(pre_grad, axis=0)[None],
+            second_in,
+            up_cols,
+            down_weight,
             by_block(residual),
-            by_block(grad_all),
             hidden_in,
             by_block(queries),
             by_block(key_rows),
@@ -1369,8 +1507,6 @@
             out_weight,
             by_block(first_in),
             qkv_cols,
-            vectors,
-            jnp.sum(pre_grad, axis=0)[None],
         ),
         sum(lengths_out),
     )
@@ -1401,6 +1537,14 @@
     )
 
 
+def layer_rows(vectors, count):
+    place = lax.broadcasted_iota(jnp.int32, (count, vectors[0].shape[0]), 0)
+    rows = jnp.zeros(place.shape, vectors[0].dtype)
+    for i, vector in enumerate(vectors):
+        rows = jnp.where(place == i, vector[None], rows)
+    return rows
+
+
 def attend_kernel(q_ref, k_ref, v_ref, allow_ref, ctx_ref):
     rows, band = q_ref.shape[1:]
     lane = lax.broadcasted_iota(jnp.int32, (rows, 128), 1)
@@ -1410,16 +1554,25 @@
     @pl.loop(0, q_ref.shape[0])
     def _(block):
         visible = allow_ref[block] > 0.5
-        for pair in range(band // 128):
-            cut = slice(pair * 128, (pair + 1) * 128)
-            query, key, value = q_ref[block, :, cut], k_ref[block, :, cut], v_ref[block, :, cut]
-            parts = []
-            for mask in masks:
-                scores = right_product(query * mask, key) * (1.0 / math.sqrt(HEAD_DIM))
-                total = jnp.sum(jnp.where(visible, jnp.exp(scores), 0.0), axis=-1, keepdims=True)
-                probs = jnp.where(visible, jnp.exp(scores - jnp.log(total)), 0.0)
-                parts.append(product(probs.astype(jnp.bfloat16), value))
-            ctx_ref[block, :, cut] = jnp.where(sides[0], parts[0], parts[1]).astype(jnp.bfloat16)
+        cuts = [slice(pair * 128, (pair + 1) * 128) for pair in range(band // 128)]
+        scores = [
+            right_product(q_ref[block, :, cut] * mask, k_ref[block, :, cut])
+            * (1.0 / math.sqrt(HEAD_DIM))
+            for cut in cuts
+            for mask in masks
+        ]
+        totals = [
+            jnp.sum(jnp.where(visible, jnp.exp(score), 0.0), axis=-1, keepdims=True) for score in scores
+        ]
+        probs = [
+            jnp.where(visible, jnp.exp(score - jnp.log(total)), 0.0).astype(jnp.bfloat16)
+            for score, total in zip(scores, totals)
+        ]
+        for i, cut in enumerate(cuts):
+            value = v_ref[block, :, cut]
+            ctx_ref[block, :, cut] = jnp.where(
+                sides[0], product(probs[2 * i], value), product(probs[2 * i + 1], value)
+            ).astype(jnp.bfloat16)
 
 
 def attend(queries, key_rows, values, allow):
@@ -1435,7 +1588,7 @@
     rows, width = hidden_in.shape
     band = width // size
     aligned = width % size == 0 and band % 256 == 0 and band % (16 * ring) == 0
-    body = fused if aligned and rows % 128 == 0 and size % 2 == 0 and ring % 2 == 0 else local
+    body = fused if aligned and rows % 128 == 0 and size % 2 == 0 and ring % 4 == 0 else local
     return body(ring, size, hidden_in, *rest)
 
 

time: 286 us -> 253 us (0.88)
  Pallas kernels: 231 us -> 210 us
  matrix products: 18.1 us -> 10 us
  local copies, waits for them, and re-layouts: 13.4 us -> 6.07 us
  other arithmetic: 21.3 us -> 24.8 us
    pallas_call x1, Pallas kernels: 162 us -> 146 us  [back(): pl.pallas_call(functools.partial(back_kernel, size, ring), out_shape=outs...]
    unnamed x35 -> x32, local copies, waits for them, and re-layouts: 8.36 us -> 2.65 us
    dot_general x2 -> x0, matrix products: 5.58 us -> none  [left_product(): lax.dot_general(left, right, (((0,), (0,)), ((), ())), preferred_element_...]
    pallas_call x1, Pallas kernels: 6.61 us -> 3.69 us  [attend(): pl.pallas_call(attend_kernel, out_shape=jax.ShapeDtypeStruct(queries.shap...]
    dot_general x4 -> x3, matrix products: 7.28 us -> 6.04 us  [product(): return jnp.dot(left, right, preferred_element_type=jnp.float32)]
where the time goes in v1:
time: 253 us; the launch traced here: 252 us
  Pallas kernels  210 us (83%)
  other arithmetic  24.8 us (10%)
  matrix products  10 us (4%)
  local copies, waits for them, and re-layouts  6.07 us (2%)
    pallas_call x1, Pallas kernels, back(): pl.pallas_call(functools.partial(back_kernel, size, ring), out_shape=outs...  146 us
    pallas_call x1, Pallas kernels, entry(): pl.pallas_call(functools.partial(entry_kernel, size, (3, 1)), out_shape=o...  39.1 us
    pallas_call x1, Pallas kernels, group_sum(): pl.pallas_call(functools.partial(group_sum_kernel, size, gathers), out_sh...  21.4 us
    convert_element_type x4, other arithmetic, fused(): final = lambda array, like: array.reshape(like.shape).astype(jnp.float32)  9.51 us
    dot_general x3, matrix products, product(): return jnp.dot(left, right, preferred_element_type=jnp.float32)  6.04 us

profile of v1, /device:TPU:0, one launch (start us, length us, event | category | flops | bytes accessed | tf_op | source)
XLA Modules:
  0.0 252.1 jit_solution(9912167536490147497)
XLA Ops:
  0.6 0.7 convert_bitcast_fusion
  1.3 0.7 convert_element_type.174
  2.0 0.7 convert_element_type.176
  2.7 1.4 select_select_fusion.1.par_ref
  4.1 0.7 convert_element_type.190
  4.8 39.1 %shard_map.271 = (bf16[4,128,1024]{2,1,0:T(8,128)(2,1)}, bf16[4,128,1024]{2,1,0:T(8,128)(2,1)}, bf16[4,8,256]{2,1,0:T(8,128)(2,1)}, bf16[4,4,64,768]{3,2,1,0:T(8,128)(2,1)}, bf16[4,4,64,1024]{3,2,1,0:T(8,128)(2,1)}) custom-call(bf16[1,128,1024]{2,1,0:T(8,128)(2,1)} %bitcast.85, bf16[1,128,1024]{2,1,0:T(8,128)(2,1)} %bitcast.87, ...), custom_call_target="tpu_custom_call" | custom-call | tf_op jit(solution)/shard_map/pallas_call | solution.py:797
  43.9 0.0 copy-start.2
  43.9 0.0 copy-start.14
  43.9 0.0 copy-start.1
  43.9 0.9 slice_convert_fusion.7
  44.8 0.2 reduce_window_sum.17
  45.0 0.1 convert_reduce_fusion.2
  45.1 1.4 convert_reduce_fusion
  46.5 1.8 fusion.2
  48.3 0.0 copy-done.2
  48.3 0.2 convert_reduce_fusion.1
  48.5 0.0 copy-done.14
  48.5 0.7 select_select_fusion.vec_ref
  49.2 0.8 and_convert_fusion.allow_ref.allow_hbm
  50.0 0.0 copy-done.1
  50.0 0.4 fusion.5.first_hbm
  50.5 0.0 copy-start.4
  50.5 0.0 copy-done.10
  50.5 1.0 fusion.24
  51.5 0.0 copy-start.7
  51.5 0.7 slice.130
  52.2 0.9 fusion.17
  53.1 3.7 %shard_map.272.ctx_hbm = bf16[4,128,256]{2,1,0:T(8,128)(2,1)} custom-call(bf16[4,128,256]{2,1,0:T(8,128)(2,1)} %bitcast.77, bf16[4,128,256]{2,1,0:T(8,128)(2,1)} %bitcast.73, bf16[4,128,256]{2,1,0:T(8,128)(2,1)} %bitcast.75, f32[4,128,128]{2,1,0:T(8,128)} %and_convert_fusion.allow_ref.allow_hbm), custom_call_target="tpu_custom_call" | custom-call | tf_op jit(solution)/shard_map/pallas_call | solution.py:1579
  56.8 2.4 convolution_convert_fusion
  59.2 21.4 %shard_map.273 = bf16[4,128,1024]{2,1,0:T(8,128)(2,1)} custom-call(bf16[4,128,1024]{2,1,0:T(8,128)(2,1)} %bitcast.71), custom_call_target="tpu_custom_call" | custom-call | tf_op jit(solution)/shard_map/pallas_call | solution.py:375
  80.6 1.6 fusion.21
  82.3 0.3 multiply_reduce_fusion
  82.6 1.4 fusion.16.sec_hbm
  84.1 0.4 add_convert_fusion
  84.5 1.2 copy-done.9
  85.6 2.7 %multiply_convert_fusion = (bf16[512,1024]{1,0:T(8,128)(2,1)}, f32[512,1024]{1,0:T(8,128)S(1)}) fusion(f32[1024]{0:T(1024)S(1)} %convert_element_type.190, bf16[512,1024]{1,0:T(8,128)(2,1)S(1)} %bitcast.86, bf16[1024,1024]{1,0:T(8,128)(2,1)S(1)} %bitcast.81), kind=kOutput, calls=%fused_computation.26 | convolution fusion | flops 1078984704 | bytes 6295552 | tf_op jit(solution)/shard_map/dot_general | solution.py:21
  88.3 4.0 %fusion.22 = (f32[1024]{0:T(1024)}, bf16[512,1024]{1,0:T(8,128)(2,1)}) fusion(f32[512,1024]{1,0:T(8,128)S(1)} %get-tuple-element.65, f32[1024]{0:T(1024)S(1)} %convert_element_type.190, bf16[512,1024]{1,0:T(8,128)(2,1)S(1)} %bitcast.69, bf16[1024,1024]{1,0:T(8,128)(2,1)S(1)} %copy-done.8), kind=kOutput, calls=%fused_computation.66 | convolution fusion | flops 1084750848 | bytes 6299648 | tf_op jit(solution)/shard_map/dot_general | solution.py:31
  92.3 146.1 %shard_map.274 = (bf16[128,1024]{1,0:T(8,128)(2,1)}, bf16[128,1024]{1,0:T(8,128)(2,1)}, bf16[8,128,1024]{2,1,0:T(8,128)(2,1)}, bf16[8,32,1024]{2,1,0:T(8,128)(2,...) custom-call(bf16[512,1024]{1,0:T(8,128)(2,1)} %get-tuple-element.64.act_ref, ...), custom_call_target="tpu_custom_call" | custom-call | tf_op jit(solution)/shard_map/pallas_call | solution.py:1392
  238.4 1.4 slice.109
  239.8 1.3 fusion.23
  241.1 2.1 bitcast_convert_fusion.3
  243.2 2.1 bitcast_convert_fusion.2
  245.4 2.6 %bitcast_convert_fusion.1 = f32[256,4096]{1,0:T(8,128)} fusion(bf16[8,32,4096]{2,1,0:T(8,128)(2,1)S(1)} %copy-done.6), kind=kLoop, calls=%fused_computation.18 | loop fusion | flops 1048576 | bytes 6291456 | tf_op jit(solution)/shard_map/convert_element_type | solution.py:1513
  248.0 0.0 copy-done.5
  248.0 2.6 %bitcast_convert_fusion = f32[1024,1024]{1,0:T(8,128)} fusion(bf16[8,128,1024]{2,1,0:T(8,128)(2,1)S(1)} %copy-done.5), kind=kLoop, calls=%fused_computation.17 | loop fusion | flops 1048576 | bytes 6291456 | tf_op jit(solution)/shard_map/convert_element_type | solution.py:1513
  250.6 0.7 copy.33
  251.4 0.0 copy-done.12
  251.4 0.7 copy.34
  (29 shorter events, 0.1 us)
Async XLA Ops:
  43.9 4.4 %copy-start.2 = (bf16[4,128,1024]{2,1,0:T(8,128)(2,1)S(1)}, bf16[4,128,1024]{2,1,0:T(8,128)(2,1)}, u32[]{:S(2)}) copy-start(bf16[4,128,1024]{2,1,0:T(8,128)(2,1)} %get-tuple-element.31.grad_ref) | copy-start | bytes 3145732
  43.9 4.5 %copy-start.14 = (bf16[4,8,256]{2,1,0:T(8,128)(2,1)S(1)}, bf16[4,8,256]{2,1,0:T(8,128)(2,1)}, u32[]{:S(2)}) copy-start(bf16[4,8,256]{2,1,0:T(8,128)(2,1)} %get-tuple-element.28) | copy-start | bytes 49156
  43.9 6.1 %copy-start.1 = (bf16[4,128,1024]{2,1,0:T(8,128)(2,1)S(1)}, bf16[4,128,1024]{2,1,0:T(8,128)(2,1)}, u32[]{:S(2)}) copy-start(bf16[4,128,1024]{2,1,0:T(8,128)(2,1)} %get-tuple-element.27) | copy-start | bytes 3145732
  46.5 4.0 %copy-start.10 = (bf16[4,4,64,768]{3,2,1,0:T(8,128)(2,1)S(1)}, bf16[4,4,64,768]{3,2,1,0:T(8,128)(2,1)}, u32[]{:S(2)}) copy-start(bf16[4,4,64,768]{3,2,1,0:T(8,128)(2,1)} %get-tuple-element.29) | copy-start | bytes 4718596
  50.5 1.0 copy-start.4
  51.5 5.3 %copy-start.7 = (bf16[256,1024]{1,0:T(8,128)(2,1)S(1)}, bf16[256,1024]{1,0:T(8,128)(2,1)}, u32[]{:S(2)}) copy-start(bf16[256,1024]{1,0:T(8,128)(2,1)} %outw_hbm.1) | copy-start | bytes 1572868
  82.2 1.8 copy-start
  84.0 1.6 copy-start.9
  85.6 2.7 %copy-start.3 = (bf16[4,128,1024]{2,1,0:T(8,128)(2,1)S(1)}, bf16[4,128,1024]{2,1,0:T(8,128)(2,1)}, u32[]{:S(2)}) copy-start(bf16[4,128,1024]{2,1,0:T(8,128)(2,1)} %get-tuple-element.31.grad_ref) | copy-start | bytes 3145732
  85.6 2.7 %copy-start.8 = (bf16[1024,1024]{1,0:T(8,128)(2,1)S(1)}, bf16[1024,1024]{1,0:T(8,128)(2,1)}, u32[]{:S(2)}) copy-start(bf16[1024,1024]{1,0:T(8,128)(2,1)} %dnw_hbm.1) | copy-start | bytes 6291460
  238.4 4.8 %copy-start.11 = (bf16[8,32,3072]{2,1,0:T(8,128)(2,1)S(1)}, bf16[8,32,3072]{2,1,0:T(8,128)(2,1)}, u32[]{:S(2)}) copy-start(bf16[8,32,3072]{2,1,0:T(8,128)(2,1)} %get-tuple-element.35) | copy-start | bytes 4718596
  243.2 2.1 copy-start.6
  245.4 2.6 %copy-start.5 = (bf16[8,128,1024]{2,1,0:T(8,128)(2,1)S(1)}, bf16[8,128,1024]{2,1,0:T(8,128)(2,1)}, u32[]{:S(2)}) copy-start(bf16[8,128,1024]{2,1,0:T(8,128)(2,1)} %get-tuple-element.38) | copy-start | bytes 6291460
  248.0 2.6 %copy-start.13 = (bf16[128,1024]{1,0:T(8,128)(2,1)S(1)}, bf16[128,1024]{1,0:T(8,128)(2,1)}, u32[]{:S(2)}) copy-start(bf16[128,1024]{1,0:T(8,128)(2,1)} %get-tuple-element.88) | copy-start | bytes 786436
  248.0 3.3 %copy-start.12 = (bf16[128,1024]{1,0:T(8,128)(2,1)S(1)}, bf16[128,1024]{1,0:T(8,128)(2,1)}, u32[]{:S(2)}) copy-start(bf16[128,1024]{1,0:T(8,128)(2,1)} %get-tuple-element.89) | copy-start | bytes 786436

commit v2 on v1

--- a/solution.py
+++ b/solution.py
@@ -721,10 +721,6 @@
         Spread(out, replica, me, size, g_send.at[i], g_recv.at[i])
         for i, out in enumerate((hid_out, grad_out, par_out))
     ]
-    own[0].wait()
-    own[2].wait()
-    spreads[2].start()
-    spreads[0].start()
     remote = []
     for k in range(1, half):
         j = lax.rem(outer + k, half)
@@ -745,10 +741,9 @@
             )
             copy.start()
             first.append(copy)
-    own[1].wait()
-    spreads[1].start()
-    spreads[2].forward()
-    spreads[0].forward()
+    for i in (2, 0, 1):
+        own[i].wait()
+        spreads[i].start()
     second = []
     for w in range(2):
         dst = weights[w][1]
@@ -764,7 +759,8 @@
                 )
                 copy.start()
                 second.append(copy)
-    spreads[1].forward()
+    for i in (2, 0, 1):
+        spreads[i].forward()
     for w in range(2):
         dst = weights[w][1]
         for source in remote:
@@ -1442,25 +1438,15 @@
     gain_one, bias_one, outb_full, gain_two, bias_two, downb_full = (
         params_all[:, i, :band].reshape(width) for i in range(6)
     )
-    lengths_all = params_all[:, 6, :seqs].astype(jnp.int32)
-
-    allowed = seq_mask(lengths_all, rows)
     inputs_wide = hidden_all.astype(jnp.float32)
     first_out, _, _ = layer_norm(inputs_wide, gain_one, bias_one)
     first_in = first_out.astype(jnp.bfloat16)
     projected = product(first_in, qkv_cols)
-    queries = (projected[:, :band] + query_bias.astype(jnp.float32)).astype(jnp.bfloat16)
-    key_rows = projected[:, band : 2 * band].astype(jnp.bfloat16)
-    values = (projected[:, 2 * band :] + value_bias.astype(jnp.float32)).astype(jnp.bfloat16)
     by_block = lambda array: array.reshape(size, rows, array.shape[-1])
-    allow = allowed.astype(jnp.float32)
-    context = attend(by_block(queries), by_block(key_rows), by_block(values), allow)
-    (attended,) = group_sum(
-        size,
-        [product(context.reshape(size * rows, band), out_weight).astype(jnp.bfloat16)],
-        (True,),
-        1,
-    )
+    queries, key_rows, values, allow, context, attend_part = attend(
+        seqs, by_block(projected), params_all, query_bias, value_bias, out_weight
+    )
+    (attended,) = group_sum(size, [attend_part], (True,), 1)
     residual = (
         inputs_wide
         + attended.reshape(size * rows, width).astype(jnp.float32)
@@ -1499,9 +1485,9 @@
             down_weight,
             by_block(residual),
             hidden_in,
-            by_block(queries),
-            by_block(key_rows),
-            by_block(values),
+            queries,
+            key_rows,
+            values,
             allow,
             context,
             out_weight,
@@ -1545,19 +1531,36 @@
     return rows
 
 
-def attend_kernel(q_ref, k_ref, v_ref, allow_ref, ctx_ref):
-    rows, band = q_ref.shape[1:]
+def attend_kernel(seqs, proj_ref, par_ref, qbias_ref, vbias_ref, outw_ref,
+                  q_out, k_out, v_out, allow_out, ctx_out, part_out):
+    rows, band = q_out.shape[1:]
     lane = lax.broadcasted_iota(jnp.int32, (rows, 128), 1)
     sides = [(lane < HEAD_DIM), (lane >= HEAD_DIM)]
     masks = [side.astype(jnp.float32).astype(jnp.bfloat16) for side in sides]
-
-    @pl.loop(0, q_ref.shape[0])
+    above = lax.broadcasted_iota(jnp.int32, (rows, rows), 0).astype(jnp.float32)
+    across = lax.broadcasted_iota(jnp.int32, (rows, rows), 1).astype(jnp.float32)
+
+    @pl.loop(0, q_out.shape[0])
     def _(block):
-        visible = allow_ref[block] > 0.5
+        line = par_ref[block].astype(jnp.float32)[6:7]
+        apart = jnp.where(across <= above, 0.0, 1.0)
+        end = jnp.zeros((1, 1), jnp.float32)
+        for m in range(seqs):
+            end = end + line[:, m : m + 1]
+            apart = apart + jnp.where(above >= end, 1.0, 0.0) - jnp.where(across >= end, 1.0, 0.0)
+        visible = (across <= above) & (apart < 0.5)
+        allow_out[block] = jnp.where(visible, 1.0, 0.0)
+        queries = (proj_ref[block, :, :band] + qbias_ref[...].astype(jnp.float32)).astype(jnp.bfloat16)
+        key_rows = proj_ref[block, :, band : 2 * band].astype(jnp.bfloat16)
+        values = (proj_ref[block, :, 2 * band :] + vbias_ref[...].astype(jnp.float32)).astype(
+            jnp.bfloat16
+        )
+        q_out[block] = queries
+        k_out[block] = key_rows
+        v_out[block] = values
         cuts = [slice(pair * 128, (pair + 1) * 128) for pair in range(band // 128)]
         scores = [
-            right_product(q_ref[block, :, cut] * mask, k_ref[block, :, cut])
-            * (1.0 / math.sqrt(HEAD_DIM))
+            right_product(queries[:, cut] * mask, key_rows[:, cut]) * (1.0 / math.sqrt(HEAD_DIM))
             for cut in cuts
             for mask in masks
         ]
@@ -1569,19 +1572,32 @@
             for score, total in zip(scores, totals)
         ]
         for i, cut in enumerate(cuts):
-            value = v_ref[block, :, cut]
-            ctx_ref[block, :, cut] = jnp.where(
+            value = values[:, cut]
+            ctx_out[block, :, cut] = jnp.where(
                 sides[0], product(probs[2 * i], value), product(probs[2 * i + 1], value)
             ).astype(jnp.bfloat16)
-
-
-def attend(queries, key_rows, values, allow):
+        part_out[block] = product(ctx_out[block], outw_ref[...]).astype(jnp.bfloat16)
+
+
+def attend(seqs, projected, params_all, query_bias, value_bias, out_weight):
+    size, rows, wide = projected.shape
+    band = wide // 3
+    shape = jax.ShapeDtypeStruct
+    head = shape((size, rows, band), jnp.bfloat16)
+    outs = (
+        head,
+        head,
+        head,
+        shape((size, rows, rows), jnp.float32),
+        head,
+        shape((size, rows, out_weight.shape[1]), jnp.bfloat16),
+    )
     return pl.pallas_call(
-        attend_kernel,
-        out_shape=jax.ShapeDtypeStruct(queries.shape, queries.dtype),
-        in_specs=vmem_specs(4),
-        out_specs=vmem_specs(1)[0],
-    )(queries, key_rows, values, allow)
+        functools.partial(attend_kernel, seqs),
+        out_shape=outs,
+        in_specs=vmem_specs(5),
+        out_specs=tuple(vmem_specs(len(outs))),
+    )(projected, params_all, query_bias[None], value_bias[None], out_weight)
 
 
 def choose(ring, size, hidden_in, *rest):

time: 253 us -> 246 us (0.972)
  Pallas kernels: 210 us -> 206 us
  other arithmetic: 24.8 us -> 20.8 us
  local copies, waits for them, and re-layouts: 6.07 us -> 8.73 us
    pallas_call x1, Pallas kernels: 39.1 us -> 33.5 us  [entry(): pl.pallas_call(functools.partial(entry_kernel, size, (3, 1)), out_shape=o...]
    convert_element_type x4 -> x0, other arithmetic: 3.01 us -> none  [the longest x1 0.87 us: fused(): (projected[:, 2 * band:] + value_bias.astype(jnp.float32)).astype(jnp.bfl...]
    dot_general x3 -> x2, matrix products: 6.04 us -> 4.82 us  [product(): return jnp.dot(left, right, preferred_element_type=jnp.float32)]
where the time goes in v2:
time: 246 us
  Pallas kernels  206 us (84%)
  other arithmetic  20.8 us (8%)
  matrix products  8.79 us (4%)
  local copies, waits for them, and re-layouts  8.73 us (4%)
    pallas_call x1, Pallas kernels, back(): pl.pallas_call(functools.partial(back_kernel, size, ring), out_shape=outs...  146 us
    pallas_call x1, Pallas kernels, entry(): pl.pallas_call(functools.partial(entry_kernel, size, (3, 1)), out_shape=o...  33.5 us
    pallas_call x1, Pallas kernels, group_sum(): pl.pallas_call(functools.partial(group_sum_kernel, size, gathers), out_sh...  21.5 us
    convert_element_type x4, other arithmetic, fused(): final = lambda array, like: array.reshape(like.shape).astype(jnp.float32)  9.51 us
    pallas_call x1, Pallas kernels, attend(): pl.pallas_call(functools.partial(attend_kernel, seqs), out_shape=outs, in...  5.27 us

profile of v2, /device:TPU:0, one launch (start us, length us, event | category | flops | bytes accessed | tf_op | source)
XLA Modules:
  0.0 245.5 jit_solution(10139200371776650484)
XLA Ops:
  0.6 0.7 convert_bitcast_fusion
  1.3 1.2 broadcast_in_dim.114.qbias_ref
  2.5 1.2 broadcast_in_dim.115.vbias_ref
  3.8 1.4 select_select_fusion.1.par_ref
  5.2 0.7 convert_element_type.156
  5.9 33.5 %shard_map.271 = (bf16[4,128,1024]{2,1,0:T(8,128)(2,1)}, bf16[4,128,1024]{2,1,0:T(8,128)(2,1)}, bf16[4,8,256]{2,1,0:T(8,128)(2,1)}, bf16[4,4,64,768]{3,2,1,0:T(8,128)(2,1)}, bf16[4,4,64,1024]{3,2,1,0:T(8,128)(2,1)}) custom-call(bf16[1,128,1024]{2,1,0:T(8,128)(2,1)} %bitcast.69, bf16[1,128,1024]{2,1,0:T(8,128)(2,1)} %bitcast.71, ...), custom_call_target="tpu_custom_call" | custom-call | tf_op jit(solution)/shard_map/pallas_call | solution.py:793
  39.4 0.0 copy-start.2
  39.4 0.0 copy-start.13
  39.4 0.0 copy-start.1
  39.4 1.6 convert_reduce_fusion
  41.0 1.8 fusion.2
  42.8 0.0 copy-done.2
  42.8 0.2 convert_reduce_fusion.1
  43.0 0.0 copy-done.13
  43.0 0.7 select_select_fusion.vec_ref
  43.7 0.0 copy-done.1
  43.7 0.4 fusion.5.first_hbm
  44.1 0.0 copy-start.4
  44.1 1.0 copy-done.4
  45.1 0.0 copy-done.9
  45.1 2.1 fusion.22.proj_ref
  47.2 5.3 %shard_map.272 = (bf16[4,128,256]{2,1,0:T(8,128)(2,1)}, bf16[4,128,256]{2,1,0:T(8,128)(2,1)}, bf16[4,128,256]{2,1,0:T(8,128)(2,1)}, f32[4,128,128]{2,1,0:T(8,128...) custom-call(f32[4,128,768]{2,1,0:T(8,128)} %fusion.22.proj_ref, ...), custom_call_target="tpu_custom_call" | custom-call | tf_op jit(solution)/shard_map/pallas_call | solution.py:1595
  52.5 21.5 %shard_map.273 = bf16[4,128,1024]{2,1,0:T(8,128)(2,1)} custom-call(bf16[4,128,1024]{2,1,0:T(8,128)(2,1)} %get-tuple-element.36.refs_0_), custom_call_target="tpu_custom_call" | custom-call | tf_op jit(solution)/shard_map/pallas_call | solution.py:375
  74.0 1.6 fusion.19
  75.7 0.3 multiply_reduce_fusion
  76.1 1.4 fusion.16.sec_hbm
  77.5 0.0 copy-done
  77.5 0.4 add_convert_fusion
  77.9 1.2 copy-done.8
  79.1 2.7 %multiply_convert_fusion = (bf16[512,1024]{1,0:T(8,128)(2,1)}, f32[512,1024]{1,0:T(8,128)S(1)}) fusion(f32[1024]{0:T(1024)S(1)} %convert_element_type.156, bf16[512,1024]{1,0:T(8,128)(2,1)S(1)} %bitcast.70, bf16[1024,1024]{1,0:T(8,128)(2,1)S(1)} %bitcast.65), kind=kOutput, calls=%fused_computation.26 | convolution fusion | flops 1078984704 | bytes 6295552 | tf_op jit(solution)/shard_map/dot_general | solution.py:21
  81.8 0.0 copy-done.3
  81.8 0.0 copy-done.7
  81.8 4.0 %fusion.20 = (f32[1024]{0:T(1024)}, bf16[512,1024]{1,0:T(8,128)(2,1)}) fusion(f32[512,1024]{1,0:T(8,128)S(1)} %get-tuple-element.75, f32[1024]{0:T(1024)S(1)} %convert_element_type.156, bf16[512,1024]{1,0:T(8,128)(2,1)S(1)} %bitcast.62, bf16[1024,1024]{1,0:T(8,128)(2,1)S(1)} %copy-done.7), kind=kOutput, calls=%fused_computation.55 | convolution fusion | flops 1084750848 | bytes 6299648 | tf_op jit(solution)/shard_map/dot_general | solution.py:31
  85.8 146.1 %shard_map.274 = (bf16[128,1024]{1,0:T(8,128)(2,1)}, bf16[128,1024]{1,0:T(8,128)(2,1)}, bf16[8,128,1024]{2,1,0:T(8,128)(2,1)}, bf16[8,32,1024]{2,1,0:T(8,128)(2,...) custom-call(bf16[512,1024]{1,0:T(8,128)(2,1)} %get-tuple-element.74.act_ref, ...), custom_call_target="tpu_custom_call" | custom-call | tf_op jit(solution)/shard_map/pallas_call | solution.py:1388
  231.9 0.0 copy-start.10
  231.9 1.4 slice.92
  233.3 1.3 fusion.21
  234.6 2.1 bitcast_convert_fusion.3
  236.7 0.0 copy-done.10
  236.7 2.1 bitcast_convert_fusion.2
  238.8 0.0 copy-done.6
  238.8 2.6 %bitcast_convert_fusion.1 = f32[256,4096]{1,0:T(8,128)} fusion(bf16[8,32,4096]{2,1,0:T(8,128)(2,1)S(1)} %copy-done.6), kind=kLoop, calls=%fused_computation.18 | loop fusion | flops 1048576 | bytes 6291456 | tf_op jit(solution)/shard_map/convert_element_type | solution.py:1499
  241.5 0.0 copy-done.5
  241.5 2.6 %bitcast_convert_fusion = f32[1024,1024]{1,0:T(8,128)} fusion(bf16[8,128,1024]{2,1,0:T(8,128)(2,1)S(1)} %copy-done.5), kind=kLoop, calls=%fused_computation.17 | loop fusion | flops 1048576 | bytes 6291456 | tf_op jit(solution)/shard_map/convert_element_type | solution.py:1499
  244.1 0.0 copy-done.12
  244.1 0.7 copy.33
  244.8 0.0 copy-done.11
  244.8 0.7 copy.34
  (19 shorter events, 0.1 us)
Async XLA Ops:
  39.4 3.4 %copy-start.2 = (bf16[4,128,1024]{2,1,0:T(8,128)(2,1)S(1)}, bf16[4,128,1024]{2,1,0:T(8,128)(2,1)}, u32[]{:S(2)}) copy-start(bf16[4,128,1024]{2,1,0:T(8,128)(2,1)} %get-tuple-element.38.grad_ref) | copy-start | bytes 3145732
  39.4 3.6 %copy-start.13 = (bf16[4,8,256]{2,1,0:T(8,128)(2,1)S(1)}, bf16[4,8,256]{2,1,0:T(8,128)(2,1)}, u32[]{:S(2)}) copy-start(bf16[4,8,256]{2,1,0:T(8,128)(2,1)} %get-tuple-element.34.par_ref) | copy-start | bytes 49156
  39.4 4.3 %copy-start.1 = (bf16[4,128,1024]{2,1,0:T(8,128)(2,1)S(1)}, bf16[4,128,1024]{2,1,0:T(8,128)(2,1)}, u32[]{:S(2)}) copy-start(bf16[4,128,1024]{2,1,0:T(8,128)(2,1)} %get-tuple-element.33) | copy-start | bytes 3145732
  41.0 4.1 %copy-start.9 = (bf16[4,4,64,768]{3,2,1,0:T(8,128)(2,1)S(1)}, bf16[4,4,64,768]{3,2,1,0:T(8,128)(2,1)}, u32[]{:S(2)}) copy-start(bf16[4,4,64,768]{3,2,1,0:T(8,128)(2,1)} %get-tuple-element.35) | copy-start | bytes 4718596
  44.1 1.0 copy-start.4
  75.7 1.8 copy-start
  77.5 1.6 copy-start.8
  79.1 2.7 %copy-start.3 = (bf16[4,128,1024]{2,1,0:T(8,128)(2,1)S(1)}, bf16[4,128,1024]{2,1,0:T(8,128)(2,1)}, u32[]{:S(2)}) copy-start(bf16[4,128,1024]{2,1,0:T(8,128)(2,1)} %get-tuple-element.38.grad_ref) | copy-start | bytes 3145732
  79.1 2.7 %copy-start.7 = (bf16[1024,1024]{1,0:T(8,128)(2,1)S(1)}, bf16[1024,1024]{1,0:T(8,128)(2,1)}, u32[]{:S(2)}) copy-start(bf16[1024,1024]{1,0:T(8,128)(2,1)} %dnw_hbm.1) | copy-start | bytes 6291460
  231.9 4.8 %copy-start.10 = (bf16[8,32,3072]{2,1,0:T(8,128)(2,1)S(1)}, bf16[8,32,3072]{2,1,0:T(8,128)(2,1)}, u32[]{:S(2)}) copy-start(bf16[8,32,3072]{2,1,0:T(8,128)(2,1)} %get-tuple-element.47) | copy-start | bytes 4718596
  236.7 2.1 copy-start.6
  238.8 2.6 %copy-start.5 = (bf16[8,128,1024]{2,1,0:T(8,128)(2,1)S(1)}, bf16[8,128,1024]{2,1,0:T(8,128)(2,1)}, u32[]{:S(2)}) copy-start(bf16[8,128,1024]{2,1,0:T(8,128)(2,1)} %get-tuple-element.50) | copy-start | bytes 6291460
  241.5 2.6 %copy-start.12 = (bf16[128,1024]{1,0:T(8,128)(2,1)S(1)}, bf16[128,1024]{1,0:T(8,128)(2,1)}, u32[]{:S(2)}) copy-start(bf16[128,1024]{1,0:T(8,128)(2,1)} %get-tuple-element.98) | copy-start | bytes 786436
  241.5 3.3 %copy-start.11 = (bf16[128,1024]{1,0:T(8,128)(2,1)S(1)}, bf16[128,1024]{1,0:T(8,128)(2,1)}, u32[]{:S(2)}) copy-start(bf16[128,1024]{1,0:T(8,128)(2,1)} %get-tuple-element.99) | copy-start | bytes 786436
